TPU v7x, 128 devices: a whole 4x4x4 slice. The times are simulated.
128 devices in a mesh: dp: 8 (over z_lo, y), tensor: 16 (over x, z_hi, core).
Axes of the slice: x: 4, y: 4, z: 4 (z_hi: 2, z_lo: 2; z = z_hi * 2 + z_lo), core: 2. Of those that a mesh axis runs over, the one named last changes fastest.
Arguments:
- token_ids: int32 [1024], replicated, may hold values from 0 to 15999
- old_embed: bfloat16 [16000, 5120], P('tensor', 'dp'), as said below
- expand_in: bfloat16 [8192, 5120], P('dp'), may hold values from -0.078125 to 0.078125
- query_out: bfloat16 [4096, 5120], P('tensor'), may hold values from -0.078125 to 0.078125
- key_out: bfloat16 [4096, 5120], P('tensor'), may hold values from -0.078125 to 0.078125
- old_query: bfloat16 [5120, 5120], P('dp', 'tensor'), may hold values from -0.078125 to 0.078125
- old_key: bfloat16 [5120, 5120], P('dp', 'tensor'), may hold values from -0.078125 to 0.078125
Outputs:
- grown_embedding: bfloat16 [16000, 8192], P('tensor', 'dp')
- grown_query: bfloat16 [8192, 4096], P('dp', 'tensor')
- grown_key: bfloat16 [8192, 4096], P('dp', 'tensor')
- attention_entropy: float32 [1024, 32], P('dp', 'tensor')
Inputs may be any that keep to these rules, and one draw needn't show every extreme that they name: `old_embed`: old embedding rows and features carry independent scales.
All inputs are finite; a program needn't handle non-finite values.
Results may differ from a plain program's by a relative error of at most 0.0097.
Values may be sent and summed in bfloat16 or wider, within the bound.
A program may use at most 128 MiB of HBM per device.

v0:
```python
import math

import jax
import jax.numpy as jnp
from jax import lax
from jax.sharding import PartitionSpec as P

D_NEW = 8192
HEAD = 128


EMBED_EPSILON = 1e-06
TOKEN_EPSILON = 1e-05


def contract_last(left_side, right_side):
    return lax.dot_general(
        left_side, right_side, (((1,), (1,)), ((), ())), preferred_element_type=jnp.float32
    )


def rotate(values, head_count):
    row_count = values.shape[0]
    shaped = values.reshape(row_count, head_count, HEAD)
    half_size = HEAD // 2
    position = jnp.arange(row_count).astype(jnp.float32)
    frequency = jnp.exp(
        -math.log(10000.0) * jnp.arange(half_size).astype(jnp.float32) * (2.0 / HEAD)
    )
    angles = position[:, None] * frequency[None, :]
    cosine = jnp.cos(angles)[:, None, :]
    sine_table = jnp.sin(angles)[:, None, :]
    first_half = shaped[..., :half_size]
    second = shaped[..., half_size:]
    return jnp.concatenate(
        [first_half * cosine - second * sine_table, second * cosine + first_half * sine_table],
        axis=-1,
    )


def entropy_of(queries, key_proj, head_count):
    rotated_q = rotate(queries, head_count).astype(jnp.bfloat16)
    rotated_k = rotate(key_proj, head_count).astype(jnp.bfloat16)
    scores = jnp.einsum(
        "ihd,jhd->hij", rotated_q, rotated_k, preferred_element_type=jnp.float32
    ) * HEAD ** (-0.5)
    row_count = queries.shape[0]
    causal = jnp.arange(row_count)[:, None] >= jnp.arange(row_count)[None, :]
    weights = jnp.where(causal[None], jnp.exp(scores), 0.0)
    weight_sum = jnp.sum(weights, axis=-1)
    entropy = jnp.log(weight_sum) - jnp.sum(weights * scores, axis=-1) / weight_sum
    return entropy.T


def on_device(token_ids, old_embed, expand_in, query_out, key_out, old_query, old_key):
    vocab_rows = old_embed.shape[0]
    old_width = expand_in.shape[1]
    head_cols = query_out.shape[0]
    head_count = head_cols // HEAD
    shard_piece = lax.all_gather(old_embed, "dp", axis=1, tiled=True)
    operator_slab = expand_in
    raw_rows = contract_last(shard_piece, operator_slab)
    old_squares = jnp.sum(jnp.square(shard_piece.astype(jnp.float32)), axis=1)
    raw_rows, old_squares = (raw_rows, old_squares)
    new_squares = lax.psum(jnp.sum(jnp.square(raw_rows), axis=1), "dp")
    factor = jnp.sqrt(
        (old_squares / old_width + EMBED_EPSILON) / (new_squares / D_NEW + EMBED_EPSILON)
    )
    grown_embedding = (raw_rows * factor[:, None]).astype(jnp.bfloat16)
    pieces = (
        lax.all_gather(old_query, "tensor", axis=1, tiled=True),
        lax.all_gather(old_key, "tensor", axis=1, tiled=True),
    )
    inner_query = contract_last(query_out, pieces[0])
    inner_key = contract_last(key_out, pieces[1])
    inner_query = inner_query.astype(jnp.bfloat16)
    inner_key = inner_key.astype(jnp.bfloat16)
    pieces = (
        lax.all_gather(inner_query, "dp", axis=1, tiled=True),
        lax.all_gather(inner_key, "dp", axis=1, tiled=True),
    )
    operator_slab = expand_in
    grown_q32 = contract_last(operator_slab, pieces[0])
    grown_k32 = contract_last(operator_slab, pieces[1])
    grown_query = grown_q32.astype(jnp.bfloat16)
    grown_key = grown_k32.astype(jnp.bfloat16)
    offset_ids = token_ids - lax.axis_index("tensor") * vocab_rows
    inside = (offset_ids >= 0) & (offset_ids < vocab_rows)
    picked = jnp.take(grown_embedding, jnp.clip(offset_ids, 0, vocab_rows - 1), axis=0)
    partial_rows = jnp.where(inside[:, None], picked.astype(jnp.float32), 0.0)
    hidden_cols = lax.psum(partial_rows.astype(jnp.bfloat16), "tensor")
    token_block = lax.all_to_all(hidden_cols, "dp", split_axis=0, concat_axis=1, tiled=True)
    square_sum = jnp.sum(jnp.square(token_block.astype(jnp.float32)), axis=1)
    pieces = (
        lax.all_gather(grown_query, "dp", axis=0, tiled=True),
        lax.all_gather(grown_key, "dp", axis=0, tiled=True),
    )
    queries = jnp.dot(token_block, pieces[0], preferred_element_type=jnp.float32)
    key_proj = jnp.dot(token_block, pieces[1], preferred_element_type=jnp.float32)
    inverse_rms = lax.rsqrt(square_sum / D_NEW + TOKEN_EPSILON)
    queries = queries * inverse_rms[:, None]
    key_proj = key_proj * inverse_rms[:, None]
    attention_entropy = entropy_of(queries, key_proj, head_count)
    return (grown_embedding, grown_query, grown_key, attention_entropy)


def solution(mesh):
    placed = (
        P(),
        P("tensor", "dp"),
        P("dp", None),
        P("tensor", None),
        P("tensor", None),
        P("dp", "tensor"),
        P("dp", "tensor"),
    )
    return jax.shard_map(
        on_device,
        mesh=mesh,
        in_specs=placed,
        out_specs=(P("tensor", "dp"), P("dp", "tensor"), P("dp", "tensor"), P("dp", "tensor")),
        check_vma=False,
    )
```

profile of v0, /device:TPU:0, one launch (start us, length us, event | category | flops | bytes accessed | tf_op | source)
XLA Modules:
  0.0 622.3 jit_solution(14580035836565688100)
XLA Ops:
  7.2 0.0 all-gather.14.cloned.1.call-start
  7.2 0.7 all-gather.14.cloned.1.call-update
  7.9 0.0 all-gather.10.cloned.1.call-start
  8.0 0.7 all-gather.10.cloned.1.call-update
  8.7 0.0 all-gather.8.cloned.1.call-start
  8.7 0.7 all-gather.8.cloned.1.call-update
  9.4 0.0 all-gather.16.cloned.1.call-start
  9.4 68.4 %all-gather.14.cloned.1.call-done = bf16[640,5120]{0,1:T(8,128)(2,1)} async-done(((bf16[640,320]{0,1:T(8,128)(2,1)}), bf16[640,5120]{0,1:T(8,128)(2,1)}) %all-gather.14.cloned.1.call-update) | async-done | bytes 6553616 | tf_op jit(solution)/shard_map/all_gather | solution.py:72
  77.9 5.8 convolution_convert_fusion.2
  83.6 0.0 all-gather.16.cloned.1.call-update
  83.7 0.0 all-gather.12.cloned.1.call-start
  83.7 59.8 %all-gather.10.cloned.1.call-done = bf16[640,5120]{0,1:T(8,128)(2,1)} async-done(((bf16[640,320]{0,1:T(8,128)(2,1)}), bf16[640,5120]{0,1:T(8,128)(2,1)}) %all-gather.10.cloned.1.call-update) | async-done | bytes 6553616 | tf_op jit(solution)/shard_map/all_gather | solution.py:71
  143.5 6.6 %convolution_convert_fusion.3 = bf16[256,640]{1,0:T(8,128)(2,1)} fusion(bf16[256,5120]{1,0:T(8,128)(2,1)} %param.10, bf16[640,5120]{0,1:T(8,128)(2,1)} %all-gather.10.cloned.1.call-done), kind=kOutput, calls=%fused_computation.11 | convolution fusion | flops 1677885440 | bytes 9502720 | tf_op jit(solution)/shard_map/dot_general | solution.py:17
  150.1 0.0 all-gather.12.cloned.1.call-update
  150.1 0.0 all-reduce.2.cloned.1.call-start
  150.2 102.6 %all-gather.8.cloned.1.call-done = bf16[1000,5120]{1,0:T(8,128)(2,1)} async-done(((bf16[1000,640]{1,0:T(8,128)(2,1)}), bf16[1000,5120]{1,0:T(8,128)(2,1)}) %all-gather.8.cloned.1.call-update) | async-done | bytes 10240016 | tf_op jit(solution)/shard_map/all_gather | solution.py:60
  252.8 17.9 %multiply_reduce_fusion.2 = (f32[1000]{0:T(1024)S(1)}, f32[1000,1024]{1,0:T(8,128)}) fusion(bf16[1000,5120]{1,0:T(8,128)(2,1)} %all-gather.8.cloned.1.call-done, bf16[1024,5120]{1,0:T(8,128)(2,1)} %param.9), kind=kOutput, calls=%fused_computation.5 | convolution fusion | flops 10487806976 | bytes 24825760 | tf_op jit(solution)/shard_map/dot_general | solution.py:17
  270.7 17.2 %psum.14 = f32[1000]{0:T(1024)S(1)} all-reduce(f32[1000]{0:T(1024)S(1)} %get-tuple-element.28), channel_id=1, replica_groups=mesh['dp'=8,'tensor'=16] {'dp'}, use_global_device_ids=true, to_apply=%region_2.0 | all-reduce | flops 1000 | bytes 8000 | tf_op jit(solution)/shard_map/psum | solution.py:65
  287.9 6.2 multiply_reduce_fusion
  294.2 0.3 multiply_convert_fusion
  294.5 5.4 gather_fusion
  299.8 2.2 select_convert_fusion
  302.0 2.4 copy.17
  304.4 0.0 all-reduce.2.cloned.1.call-update
  304.5 0.0 all-gather.20.cloned.1.call-start
  304.5 0.0 all-gather.16.cloned.1.call-done
  304.5 8.6 %fusion.1 = bf16[1024,256]{0,1:T(8,128)(2,1)} fusion(bf16[256,5120]{1,0:T(8,128)(2,1)} %all-gather.16.cloned.1.call-done, bf16[1024,5120]{1,0:T(8,128)(2,1)} %param.9), kind=kOutput, calls=%fused_computation.9 | convolution fusion | flops 2684616704 | bytes 13631488 | tf_op jit(solution)/shard_map/dot_general | solution.py:17
  313.2 0.0 all-gather.20.cloned.1.call-update
  313.2 0.0 all-gather.18.cloned.1.call-start
  313.2 26.9 %all-gather.12.cloned.1.call-done = bf16[256,5120]{1,0:T(8,128)(2,1)} async-done(((bf16[256,640]{1,0:T(8,128)(2,1)}), bf16[256,5120]{1,0:T(8,128)(2,1)}) %all-gather.12.cloned.1.call-update) | async-done | bytes 2621456 | tf_op jit(solution)/shard_map/all_gather | solution.py:79
  340.2 8.5 %fusion = bf16[1024,256]{0,1:T(8,128)(2,1)} fusion(bf16[256,5120]{1,0:T(8,128)(2,1)} %all-gather.12.cloned.1.call-done, bf16[1024,5120]{1,0:T(8,128)(2,1)} %param.9), kind=kOutput, calls=%fused_computation.8 | convolution fusion | flops 2684616704 | bytes 13631488 | tf_op jit(solution)/shard_map/dot_general | solution.py:17
  348.7 139.4 %all-reduce.2.cloned.1.call-done = bf16[8,128,1024]{1,2,0:T(8,128)(2,1)} async-done(((bf16[8,128,1024]{1,2,0:T(8,128)(2,1)}), bf16[8,128,1024]{1,2,0:T(8,128)(2,1)}) %all-reduce.2.cloned.1.call-update) | async-done | bytes 2097168 | tf_op jit(solution)/shard_map/psum | solution.py:91
  488.1 4.3 all-to-all-start
  492.4 0.3 multiply_cosine_fusion
  492.7 1.0 copy.22
  493.7 1.0 copy.23
  494.7 35.1 %all-to-all-done = bf16[8,128,1024]{1,2,0:T(8,128)(2,1)S(1)} async-done(((bf16[8,128,1024]{1,2,0:T(8,128)(2,1)}), bf16[8,128,1024]{1,2,0:T(8,128)(2,1)S(1)}, u32[]{:S(2)}, u32[]{:S(2)}) %all-to-all-start) | async-done | bytes 2097184 | tf_op jit(solution)/shard_map/all_to_all | solution.py:92
  529.8 1.1 multiply_reduce_fusion.1
  530.9 27.6 %all-gather.20.cloned.1.call-done = bf16[8192,256]{0,1:T(8,128)(2,1)} async-done(((bf16[1024,256]{0,1:T(8,128)(2,1)}), bf16[8192,256]{0,1:T(8,128)(2,1)}) %all-gather.20.cloned.1.call-update) | async-done | bytes 4194320 | tf_op jit(solution)/shard_map/all_gather | solution.py:96
  558.5 3.7 convolution_multiply_fusion
  562.2 0.1 reshape.99
  562.3 47.5 %all-gather.18.cloned.1.call-done = bf16[8192,256]{0,1:T(8,128)(2,1)} async-done(((bf16[1024,256]{0,1:T(8,128)(2,1)}), bf16[8192,256]{0,1:T(8,128)(2,1)}) %all-gather.18.cloned.1.call-update) | async-done | bytes 4194320 | tf_op jit(solution)/shard_map/all_gather | solution.py:95
  609.8 4.3 convolution_multiply_fusion.1
  614.1 0.1 reshape.98
  614.2 0.3 fusion.11
  614.5 0.1 subtract_convert_fusion
  614.6 0.3 fusion.2
  614.9 0.6 subtract_bitcast_fusion
  (24 shorter events, 0.1 us)
Async XLA Ops:
  7.2 70.7 %copy-start = (bf16[256,5120]{1,0:T(8,128)(2,1)S(1)}, bf16[256,5120]{1,0:T(8,128)(2,1)}, u32[]{:S(2)}) copy-start(bf16[256,5120]{1,0:T(8,128)(2,1)} %param.11) | copy-start | bytes 7864324
  7.2 70.7 %all-gather.14.cloned.1.call-start = ((), (), s32[]{:S(2)}) async-start(), calls=%async_computation.4 | async-start | bytes 6963200 | tf_op jit(solution)/shard_map/all_gather | solution.py:72
  7.9 135.6 %all-gather.10.cloned.1.call-start = ((), (), s32[]{:S(2)}) async-start(), calls=%async_computation.2 | async-start | bytes 6963200 | tf_op jit(solution)/shard_map/all_gather | solution.py:71
  8.7 244.1 %all-gather.8.cloned.1.call-start = ((), (), s32[]{:S(2)}) async-start(), calls=%async_computation.1 | async-start | bytes 11520000 | tf_op jit(solution)/shard_map/all_gather | solution.py:60
  9.4 295.1 %all-gather.16.cloned.1.call-start = ((), (), s32[]{:S(2)}) async-start(), calls=%async_computation.5 | async-start | bytes 2949120 | tf_op jit(solution)/shard_map/all_gather | solution.py:80
  83.7 256.5 %all-gather.12.cloned.1.call-start = ((), (), s32[]{:S(2)}) async-start(), calls=%async_computation.3 | async-start | bytes 2949120 | tf_op jit(solution)/shard_map/all_gather | solution.py:79
  83.7 66.5 %copy-start.7 = (s32[1024]{0:T(1024)S(1)}, s32[1024]{0:T(1024)}, u32[]{:S(2)}) copy-start(s32[1024]{0:T(1024)} %param.7) | copy-start | bytes 12292
  150.1 337.9 %all-reduce.2.cloned.1.call-start = ((), (), s32[]{:S(2)}) async-start(), calls=%async_computation.6 | async-start | bytes 4194304 | tf_op jit(solution)/shard_map/psum | solution.py:91
  287.9 6.2 %copy-start.4 = (f32[1000,1024]{1,0:T(8,128)S(1)}, f32[1000,1024]{1,0:T(8,128)}, u32[]{:S(2)}) copy-start(f32[1000,1024]{1,0:T(8,128)} %get-tuple-element.29) | copy-start | bytes 12288004
  294.5 5.4 copy-start.2
  304.5 254.0 %all-gather.20.cloned.1.call-start = ((), (), s32[]{:S(2)}) async-start(), calls=%async_computation.8 | async-start | bytes 4718592 | tf_op jit(solution)/shard_map/all_gather | solution.py:96
  313.2 296.6 %all-gather.18.cloned.1.call-start = ((), (), s32[]{:S(2)}) async-start(), calls=%async_computation.7 | async-start | bytes 4718592 | tf_op jit(solution)/shard_map/all_gather | solution.py:95
  348.6 144.1 %copy-start.6 = (bf16[1024,256]{0,1:T(8,128)(2,1)S(1)}, bf16[1024,256]{0,1:T(8,128)(2,1)}, u32[]{:S(2)}) copy-start(bf16[1024,256]{0,1:T(8,128)(2,1)} %fusion) | copy-start | bytes 1572868
  348.7 145.1 %copy-start.5 = (bf16[1024,256]{0,1:T(8,128)(2,1)S(1)}, bf16[1024,256]{0,1:T(8,128)(2,1)}, u32[]{:S(2)}) copy-start(bf16[1024,256]{0,1:T(8,128)(2,1)} %fusion.1) | copy-start | bytes 1572868
  488.1 41.7 %all-to-all-start = ((bf16[8,128,1024]{1,2,0:T(8,128)(2,1)}), bf16[8,128,1024]{1,2,0:T(8,128)(2,1)S(1)}, u32[]{:S(2)}, u32[]{:S(2)}) async-start(bf16[8,128,1024]{1,2,0:T(8,128)(2,1)} %all-reduce.2.cloned.1.call-done), calls=%async_computation | async-start | bytes 4194304 | tf_op jit(solution)/shard_map/all_to_all | solution.py:92
  529.8 28.7 %copy-start.3 = (bf16[8,128,1024]{1,2,0:T(8,128)(2,1)}, bf16[8,128,1024]{1,2,0:T(8,128)(2,1)S(1)}, u32[]{:S(2)}) copy-start(bf16[8,128,1024]{1,2,0:T(8,128)(2,1)S(1)} %all-to-all-done) | copy-start | bytes 6291460
  562.2 53.3 %copy-start.1 = (bf16[256,5120]{1,0:T(8,128)(2,1)S(1)}, bf16[256,5120]{1,0:T(8,128)(2,1)}, u32[]{:S(2)}) copy-start(bf16[256,5120]{1,0:T(8,128)(2,1)} %param.11) | copy-start | bytes 7864324
Sparse Core Ops, SparseCore 0:
  10.4 67.4 all-gather.13
  80.2 63.2 all-gather.9
  145.2 107.5 all-gather.7
  254.9 41.1 all-gather.15
  298.1 42.0 all-gather.11
  342.5 145.4 all-reduce.1
  489.7 68.7 all-gather.19
  560.1 49.6 all-gather.17
where the time goes:
time: 623 us; the launch traced here: 622 us
  waiting for transfers between devices  509 us (82%)
  matrix products  55.7 us (9%)
  blocking collectives  17.2 us (3%)
  between operations  14.3 us (2%)
  other arithmetic  10.8 us (2%)
  local copies, waits for them, and re-layouts  10.3 us (2%)
    psum x1, waiting for transfers between devices, on_device(): hidden_cols = lax.psum(partial_rows.astype(jnp.bfloat16), 'tensor')  139 us
    all_gather x1, waiting for transfers between devices, on_device(): shard_piece = lax.all_gather(old_embed, 'dp', axis=1, tiled=True)  103 us
    all_gather x1, waiting for transfers between devices, on_device(): lax.all_gather(old_key, 'tensor', axis=1, tiled=True)  68.4 us
    all_gather x1, waiting for transfers between devices, on_device(): lax.all_gather(old_query, 'tensor', axis=1, tiled=True)  59.8 us
    all_gather x1, waiting for transfers between devices, on_device(): lax.all_gather(grown_query, 'dp', axis=0, tiled=True)  47.5 us
    dot_general x5, matrix products, contract_last(): lax.dot_general(left_side, right_side, (((1,), (1,)), ((), ())), preferre...  47.4 us
    all_to_all x1, waiting for transfers between devices, on_device(): lax.all_to_all(hidden_cols, 'dp', split_axis=0, concat_axis=1, tiled=True)  35.1 us
    all_gather x1, waiting for transfers between devices, on_device(): lax.all_gather(grown_key, 'dp', axis=0, tiled=True)  27.6 us
  transfers between devices with their start and end apart: 9, of which 8 were waited for; matrix products, arithmetic and copies ran while one was open for 11% of the time, Pallas kernels for 0%

commit v1 on v0

v1 whole, which is shorter than its diff:
```python
import heapq
import math

import jax
import jax.numpy as jnp
from jax import lax
from jax.experimental import pallas as pl
from jax.experimental.pallas import tpu as pltpu
from jax.sharding import PartitionSpec as P

D_NEW = 8192
HEAD = 128
N_DP = 8
N_TENSOR = 16

EMBED_EPSILON = 1e-06
TOKEN_EPSILON = 1e-05

MESH = pl.DeviceIdType.MESH
LAST = (((1,), (1,)), ((), ()))
VMEM_LIMIT = 66_000_000

STEP = {"y+": 1, "y-": -1, "x+": 1, "x-": -1}


class Place:
    def __init__(self):
        self.dp = lax.axis_index("dp")
        self.tensor = lax.axis_index("tensor")
        self.z_lo = self.dp // 4
        self.y = self.dp % 4
        self.x = self.tensor // 4
        self.z_hi = (self.tensor // 2) % 2
        self.core = self.tensor % 2

    def dp_at(self, rel):
        flip, shift = rel
        z_lo = 1 - self.z_lo if flip else self.z_lo
        return z_lo * 4 + (self.y + shift + 4) % 4

    def tensor_at(self, rel):
        flip, shift, core_flip = rel
        z_hi = 1 - self.z_hi if flip else self.z_hi
        core = 1 - self.core if core_flip else self.core
        return (((self.x + shift + 4) % 4) * 2 + z_hi) * 2 + core

    def across(self, link):
        if link in ("y+", "y-"):
            return (self.dp_at((0, STEP[link])), self.tensor)
        if link == "z":
            return (self.dp_at((1, 0)), self.tensor)
        if link in ("x+", "x-"):
            return (self.dp, self.tensor_at((0, STEP[link], 0)))
        if link == "h":
            return (self.dp, self.tensor_at((1, 0, 0)))
        return (self.dp, self.tensor_at((0, 0, 1)))


def seen_by_receiver(link, rel):
    if link in ("y+", "y-"):
        return (rel[0], (rel[1] - STEP[link]) % 4)
    if link == "z":
        return (1 - rel[0], rel[1])
    if link in ("x+", "x-"):
        return (rel[0], (rel[1] - STEP[link]) % 4, rel[2])
    if link == "h":
        return (1 - rel[0], rel[1], rel[2])
    return (rel[0], rel[1], 1 - rel[2])


def ring_tree(plus, minus, kind, rel, chunk, extra):
    near = (rel[0], (rel[1] - STEP[extra]) % 4) + tuple(rel[2:])
    return [(plus, kind, rel, chunk), (minus, kind, rel, chunk), (extra, kind, near, chunk)]


def gather_dp(kind, chunk, z_first, extra):
    other = "y-" if extra == "y+" else "y+"
    if z_first:
        sends = [("z", kind, (0, 0), chunk)]
        sends += ring_tree("y+", "y-", kind, (0, 0), chunk, extra)
        sends += ring_tree("y+", "y-", kind, (1, 0), chunk, other)
        return sends
    sends = ring_tree("y+", "y-", kind, (0, 0), chunk, extra)
    return sends + [("z", kind, (0, shift), chunk) for shift in (0, 1, 3, 2)]


def gather_tensor(kind, chunk, extra):
    other = "x-" if extra == "x+" else "x+"
    sends = [("h", kind, (0, 0, 0), chunk)]
    sends += ring_tree("x+", "x-", kind, (0, 0, 0), chunk, extra)
    sends += ring_tree("x+", "x-", kind, (1, 0, 0), chunk, other)
    sends += [("c", kind, (flip, shift, 0), chunk) for flip in (0, 1) for shift in (0, 1, 3, 2)]
    return sends


class Plan:
    def __init__(self, sends, megabytes, rates):
        self.sends = sends
        brought_by = {}
        for number, (link, kind, rel, chunk) in enumerate(sends):
            key = (kind, seen_by_receiver(link, rel), chunk)
            assert key not in brought_by
            brought_by[key] = number
        self.brought_by = brought_by
        self.keys = {number: key for key, number in brought_by.items()}
        self.after = {}
        self.first = []
        for number, (link, kind, rel, chunk) in enumerate(sends):
            source = brought_by.get((kind, rel, chunk))
            if source is None:
                assert not any(rel)
                self.first.append(number)
            else:
                self.after.setdefault(source, []).append(number)
        free, heap = {}, []

        def put(number, now):
            link, kind, _, chunk = sends[number]
            free[link] = max(free.get(link, 0.0), now) + megabytes[(kind, chunk)] / rates[link]
            heapq.heappush(heap, (free[link] + 1.5, number))

        for number in self.first:
            put(number, 0.0)
        self.order = []
        self.times = {}
        while heap:
            now, number = heapq.heappop(heap)
            self.order.append(number)
            self.times[number] = now
            for following in self.after.get(number, []):
                put(following, now)
        assert len(self.order) == len(sends)


RATES = {"y+": 0.0465, "y-": 0.0465, "z": 0.040, "x+": 0.0465, "x-": 0.0465, "h": 0.03, "c": 0.3}


def row_cuts(rows, pieces):
    step = -(-rows // (16 * pieces)) * 16
    return [(start, min(step, rows - start)) for start in range(0, rows, step)]


def greet(place, links):
    barrier = pltpu.get_barrier_semaphore()
    for link in links:
        pl.semaphore_signal(barrier, inc=1, device_id=place.across(link), device_id_type=MESH)
    pl.semaphore_wait(barrier, len(links))


X_CUTS = 5
X_MODES = ((True, "y+"), (True, "y-"), (True, "y+"), (False, "y+"), (False, "y-"))


def plan_first(vocab_rows, slab, out_slab, in_slab):
    cuts = row_cuts(vocab_rows, X_CUTS)
    sends = []
    for matrix in range(2):
        sends += gather_tensor("W", matrix, ("x+", "x-")[matrix])
    x_sends = []
    for chunk in (3, 4, 0, 1, 2):
        z_first, extra = X_MODES[chunk]
        x_sends += gather_dp("X", chunk, z_first, extra)
    x_sends.sort(key=lambda send: (send[0] == "z" and not X_MODES[send[3]][0]))
    sends += x_sends
    megabytes = {("X", chunk): cuts[chunk][1] * slab * 2e-6 for chunk in range(X_CUTS)}
    megabytes.update({("W", matrix): out_slab * in_slab * 2e-6 for matrix in range(2)})
    return cuts, Plan(sends, megabytes, RATES)


def first_kernel(
    plan, cuts, x_ref, w_ref, e_ref, q_ref, k_ref, raw_ref, inner_ref,
    x_all, w_all, e_all, o_all, total, send_sem, recv_sem, local_sem,
):
    place = Place()
    slab = x_ref.shape[1]
    greet(place, ("y+", "y-", "z", "x+", "x-", "h", "c"))

    def source(kind, rel, chunk):
        if kind == "X":
            start, size = cuts[chunk]
            if not any(rel):
                return x_ref.at[pl.ds(start, size), :]
            return x_all.at[place.dp_at(rel), pl.ds(start, size), :]
        if not any(rel):
            return w_ref.at[chunk]
        return w_all.at[chunk, place.tensor_at(rel)]

    def target(kind, rel, chunk):
        if kind == "X":
            start, size = cuts[chunk]
            return x_all.at[place.dp_at(rel), pl.ds(start, size), :]
        return w_all.at[chunk, place.tensor_at(rel)]

    def copy_of(number):
        link, kind, rel, chunk = plan.sends[number]
        return pltpu.make_async_remote_copy(
            src_ref=source(kind, rel, chunk),
            dst_ref=target(kind, rel, chunk),
            send_sem=send_sem.at[number],
            recv_sem=recv_sem.at[number],
            device_id=place.across(link),
            device_id_type=MESH,
        )

    def arrival_of(number):
        kind, rel, chunk = plan.keys[number]
        return pltpu.make_async_remote_copy(
            src_ref=target(kind, rel, chunk),
            dst_ref=target(kind, rel, chunk),
            send_sem=send_sem.at[number],
            recv_sem=recv_sem.at[number],
            device_id=place.across(plan.sends[number][0]),
            device_id_type=MESH,
        )

    for number in plan.first:
        copy_of(number).start()
    local = [
        pltpu.make_async_copy(x_ref, x_all.at[place.dp], local_sem.at[0]),
        pltpu.make_async_copy(w_ref.at[0], w_all.at[0, place.tensor], local_sem.at[1]),
        pltpu.make_async_copy(w_ref.at[1], w_all.at[1, place.tensor], local_sem.at[2]),
        pltpu.make_async_copy(e_ref, e_all, local_sem.at[3]),
        pltpu.make_async_copy(q_ref, o_all.at[0], local_sem.at[4]),
        pltpu.make_async_copy(k_ref, o_all.at[1], local_sem.at[5]),
    ]
    for copy in local:
        copy.start()
    for copy in local:
        copy.wait()

    tile = 256
    tiles = e_all.shape[0] // tile

    def add_raw(rel, fresh, half):
        at = place.dp_at(rel)
        columns = pl.ds(pl.multiple_of(at * slab, 128), slab)

        def body(number, _):
            rows = pl.ds(pl.multiple_of(number * tile, tile), tile)
            part = lax.dot_general(
                x_all[at], e_all[rows, columns], LAST, preferred_element_type=jnp.float32
            )
            if fresh:
                raw_ref[:, rows] = part
            else:
                raw_ref[:, rows] += part
            return 0

        lax.fori_loop(half * tiles // 2, (half + 1) * tiles // 2, body, 0)

    pair = 2 * w_all.shape[2]

    def add_inner(rel, matrix, fresh):
        chip = place.tensor_at((rel[0], rel[1], 0)) // 2
        columns = pl.ds(pl.multiple_of(chip * pair, 128), pair)
        slabs = w_all[matrix, pl.ds(chip * 2, 2)].reshape(pair, w_all.shape[3])
        part = jnp.dot(o_all[matrix, :, columns], slabs, preferred_element_type=jnp.float32)
        if fresh:
            total[matrix] = part
        else:
            total[matrix] += part

    landed = {("X", (0, 0), chunk) for chunk in range(len(cuts))}
    landed |= {("W", (0, 0, 0), matrix) for matrix in range(2)}
    waiting = []
    for rel in [(flip, shift) for flip in (0, 1) for shift in range(4)]:
        needs = {("X", rel, chunk) for chunk in range(len(cuts))}
        waiting += [(needs, ("raw", rel, half)) for half in range(2)]
    for matrix in range(2):
        for flip in (0, 1):
            for shift in range(4):
                needs = {("W", (flip, shift, core), matrix) for core in (0, 1)}
                waiting.append((needs, ("inner", (flip, shift), matrix)))
    done = set()

    def work(limit):
        for item in list(waiting):
            if limit == 0:
                return
            needs, (what, rel, which) = item
            if needs <= landed:
                waiting.remove(item)
                fresh = (what, which) not in done
                done.add((what, which))
                if what == "raw":
                    add_raw(rel, fresh, which)
                else:
                    add_inner(rel, which, fresh)
                limit -= 1

    work(1)
    for number in plan.order:
        arrival_of(number).wait_recv()
        for following in plan.after.get(number, []):
            copy_of(following).start()
        landed.add(plan.keys[number])
        work(1)
    work(-1)
    assert not waiting
    inner_ref[...] = total[...].astype(inner_ref.dtype)
    for number in range(len(plan.sends)):
        copy_of(number).wait_send()


def gather_and_grow(old_embed, expand_in, query_out, key_out, old_query, old_key):
    vocab_rows, slab = old_embed.shape
    in_slab, out_slab = old_query.shape
    head_cols = query_out.shape[0]
    turned = jnp.stack([old_query.T, old_key.T])
    cuts, plan = plan_first(vocab_rows, slab, out_slab, in_slab)
    count = len(plan.sends)
    anywhere = pl.BlockSpec(memory_space=pl.ANY)
    inside = pl.BlockSpec(memory_space=pltpu.VMEM)
    return pl.pallas_call(
        lambda *refs: first_kernel(plan, cuts, *refs),
        out_shape=(
            jax.ShapeDtypeStruct((vocab_rows, expand_in.shape[0]), jnp.float32),
            jax.ShapeDtypeStruct((2, head_cols, in_slab), jnp.bfloat16),
        ),
        in_specs=[anywhere] * 5,
        out_specs=(inside, inside),
        scratch_shapes=[
            pltpu.VMEM((N_DP, vocab_rows, slab), jnp.bfloat16),
            pltpu.VMEM((2, N_TENSOR, out_slab, in_slab), jnp.bfloat16),
            pltpu.VMEM(expand_in.shape, jnp.bfloat16),
            pltpu.VMEM((2,) + query_out.shape, jnp.bfloat16),
            pltpu.VMEM((2, head_cols, in_slab), jnp.float32),
            pltpu.SemaphoreType.DMA((count,)),
            pltpu.SemaphoreType.DMA((count,)),
            pltpu.SemaphoreType.DMA((6,)),
        ],
        compiler_params=pltpu.CompilerParams(
            collective_id=1, has_side_effects=True, vmem_limit_bytes=VMEM_LIMIT
        ),
        name="gather_and_grow",
    )(old_embed, turned, expand_in, query_out, key_out)


def contract_last(left_side, right_side):
    return lax.dot_general(left_side, right_side, LAST, preferred_element_type=jnp.float32)


def rotate(values, head_count):
    row_count = values.shape[0]
    shaped = values.reshape(row_count, head_count, HEAD)
    half_size = HEAD // 2
    position = jnp.arange(row_count).astype(jnp.float32)
    frequency = jnp.exp(
        -math.log(10000.0) * jnp.arange(half_size).astype(jnp.float32) * (2.0 / HEAD)
    )
    angles = position[:, None] * frequency[None, :]
    cosine = jnp.cos(angles)[:, None, :]
    sine_table = jnp.sin(angles)[:, None, :]
    first_half = shaped[..., :half_size]
    second = shaped[..., half_size:]
    return jnp.concatenate(
        [first_half * cosine - second * sine_table, second * cosine + first_half * sine_table],
        axis=-1,
    )


def entropy_of(queries, key_proj, head_count):
    rotated_q = rotate(queries, head_count).astype(jnp.bfloat16)
    rotated_k = rotate(key_proj, head_count).astype(jnp.bfloat16)
    scores = jnp.einsum(
        "ihd,jhd->hij", rotated_q, rotated_k, preferred_element_type=jnp.float32
    ) * HEAD ** (-0.5)
    row_count = queries.shape[0]
    causal = jnp.arange(row_count)[:, None] >= jnp.arange(row_count)[None, :]
    weights = jnp.where(causal[None], jnp.exp(scores), 0.0)
    weight_sum = jnp.sum(weights, axis=-1)
    entropy = jnp.log(weight_sum) - jnp.sum(weights * scores, axis=-1) / weight_sum
    return entropy.T


def on_device(token_ids, old_embed, expand_in, query_out, key_out, old_query, old_key):
    vocab_rows = old_embed.shape[0]
    old_width = expand_in.shape[1]
    head_cols = query_out.shape[0]
    head_count = head_cols // HEAD
    raw_rows, inner = gather_and_grow(old_embed, expand_in, query_out, key_out, old_query, old_key)
    squares = jnp.stack(
        [
            jnp.sum(jnp.square(old_embed.astype(jnp.float32)), axis=1),
            jnp.sum(jnp.square(raw_rows), axis=1),
        ]
    )
    squares = lax.psum(squares, "dp")
    factor = jnp.sqrt(
        (squares[0] / old_width + EMBED_EPSILON) / (squares[1] / D_NEW + EMBED_EPSILON)
    )
    grown_embedding = (raw_rows * factor[:, None]).astype(jnp.bfloat16)
    inner = lax.all_gather(inner, "dp", axis=2, tiled=True)
    grown_query = contract_last(expand_in, inner[0]).astype(jnp.bfloat16)
    grown_key = contract_last(expand_in, inner[1]).astype(jnp.bfloat16)
    offset_ids = token_ids - lax.axis_index("tensor") * vocab_rows
    chosen = (offset_ids[:, None] == jnp.arange(vocab_rows)[None, :]).astype(jnp.bfloat16)
    partial_rows = jnp.dot(chosen, grown_embedding, preferred_element_type=jnp.float32)
    hidden_cols = lax.psum(partial_rows.astype(jnp.bfloat16), "tensor")
    square_sum = jnp.sum(jnp.square(hidden_cols.astype(jnp.float32)), axis=1)
    queries = jnp.dot(hidden_cols, grown_query, preferred_element_type=jnp.float32)
    key_proj = jnp.dot(hidden_cols, grown_key, preferred_element_type=jnp.float32)
    both = jnp.concatenate([queries, key_proj], axis=1).astype(jnp.bfloat16)
    both = lax.psum_scatter(both, "dp", scatter_dimension=0, tiled=True).astype(jnp.float32)
    square_sum = lax.psum(square_sum, "dp")
    square_sum = lax.dynamic_slice(
        square_sum, (lax.axis_index("dp") * both.shape[0],), (both.shape[0],)
    )
    inverse_rms = lax.rsqrt(square_sum / D_NEW + TOKEN_EPSILON)
    both = both * inverse_rms[:, None]
    attention_entropy = entropy_of(both[:, :head_cols], both[:, head_cols:], head_count)
    return (grown_embedding, grown_query, grown_key, attention_entropy)


def solution(mesh):
    placed = (
        P(),
        P("tensor", "dp"),
        P("dp", None),
        P("tensor", None),
        P("tensor", None),
        P("dp", "tensor"),
        P("dp", "tensor"),
    )
    return jax.shard_map(
        on_device,
        mesh=mesh,
        in_specs=placed,
        out_specs=(P("tensor", "dp"), P("dp", "tensor"), P("dp", "tensor"), P("dp", "tensor")),
        check_vma=False,
    )
```

time: 623 us -> 345 us (0.55)
  waiting for transfers between devices: 509 us -> 163 us
  Pallas kernels: 0 us -> 87.8 us
  matrix products: 55.7 us -> 22.5 us
  blocking collectives: 17.2 us -> 39.1 us
    all_gather x7 -> x1, waiting for transfers between devices: 333 us -> 32.5 us  [on_device(): inner = lax.all_gather(inner, 'dp', axis=2, tiled=True)]
    pallas_call x0 -> x1, Pallas kernels: none -> 87.8 us  [gather_and_grow(): pl.pallas_call(lambda *refs: first_kernel(plan, cuts, *refs), out_shape=(...]
    all_to_all x1 -> x0, waiting for transfers between devices: 35.1 us -> none  [on_device(): lax.all_to_all(hidden_cols, 'dp', split_axis=0, concat_axis=1, tiled=True)]
    dot_general x7 -> x5, matrix products: 55.4 us -> 22.3 us  [the longest x2 15.3 us: contract_last(): lax.dot_general(left_side, right_side, LAST, preferred_element_type=jnp.f...]
    psum x1, waiting for transfers between devices: 139 us -> 112 us  [on_device(): hidden_cols = lax.psum(partial_rows.astype(jnp.bfloat16), 'tensor')]
    psum x1 -> x2, blocking collectives: 17.2 us -> 39.1 us  [the longest x1 20.3 us: on_device(): squares = lax.psum(squares, 'dp')]
    unnamed x8 -> x4, waiting for transfers between devices: 2.14 us -> 18.7 us
  transfers between devices with their start and end apart: 9 -> 3, of which waited for: 8 -> 3; matrix products, arithmetic and copies ran while one was open for 11% -> 8% of each run, Pallas kernels for 0% -> 0%
where the time goes in v1:
time: 345 us
  waiting for transfers between devices  163 us (47%)
  Pallas kernels  87.8 us (25%)
  blocking collectives  39.1 us (11%)
  matrix products  22.5 us (7%)
  between operations  15.8 us (5%)
  other arithmetic  10.4 us (3%)
  local copies, waits for them, and re-layouts  6.11 us (2%)
    psum x1, waiting for transfers between devices, on_device(): hidden_cols = lax.psum(partial_rows.astype(jnp.bfloat16), 'tensor')  112 us
    pallas_call x1, Pallas kernels, gather_and_grow(): pl.pallas_call(lambda *refs: first_kernel(plan, cuts, *refs), out_shape=(...  87.8 us
    all_gather x1, waiting for transfers between devices, on_device(): inner = lax.all_gather(inner, 'dp', axis=2, tiled=True)  32.5 us
    psum x1, blocking collectives, on_device(): squares = lax.psum(squares, 'dp')  20.3 us
    psum x1, blocking collectives, on_device(): square_sum = lax.psum(square_sum, 'dp')  18.8 us
    unnamed x4, waiting for transfers between devices  18.7 us
    dot_general x2, matrix products, contract_last(): lax.dot_general(left_side, right_side, LAST, preferred_element_type=jnp.f...  15.3 us
  transfers between devices with their start and end apart: 3, of which 3 were waited for; matrix products, arithmetic and copies ran while one was open for 8% of the time, Pallas kernels for 0%

profile of v1, /device:TPU:0, one launch (start us, length us, event | category | flops | bytes accessed | tf_op | source)
XLA Modules:
  0.0 345.0 jit_solution(5786387703093642590)
XLA Ops:
  8.0 0.0 all-gather.2.cloned.1.call-start
  8.0 2.1 pad_maximum_fusion.1.refs_1_
  10.1 87.8 %gather_and_grow.1 = (f32[1000,1024]{1,0:T(8,128)}, bf16[2,256,640]{2,1,0:T(8,128)(2,1)}) custom-call(bf16[1000,640]{1,0:T(8,128)(2,1)} %refs_0_.1, bf16[2,320,640]{2,1,0:T(8,128)(2,1)} %pad_maximum_fusion.1.refs_1_, bf16[1024,5120]{1,0:T(8,128)(2,1)} %refs_2_.1, bf16[256,5120]{1,0:T(8,128)(2,1)} %refs_3_.1, bf16[256,5120]{1,0:T(8,128)(2,1)} %refs_4_.1), custom_call_target="tpu_custom_call" | custom-call | tf_op jit(solution)/shard_map/gather_and_grow/pallas_call | solution.py:314
  98.0 0.0 all-gather.2.cloned.1.call-update
  98.0 0.0 all-reduce.2.cloned.1.call-start
  98.0 0.0 copy-start.6
  98.1 1.6 multiply_reduce_fusion.2
  99.7 2.5 multiply_reduce_fusion.1
  102.2 20.3 %psum.21 = f32[2,1000]{1,0:T(2,128)S(1)} all-reduce(f32[2,1000]{1,0:T(2,128)S(1)} %pad_maximum_fusion.2), channel_id=1, replica_groups=mesh['dp'=8,'tensor'=16] {'dp'}, use_global_device_ids=true, to_apply=%region_2.0 | all-reduce | flops 2000 | bytes 16000 | tf_op jit(solution)/shard_map/psum | solution.py:388
  122.6 0.0 copy-done.6
  122.6 2.5 multiply_convert_fusion
  125.1 0.0 copy-start.1
  125.1 1.3 copy-done.1
  126.4 3.8 %fusion.4 = bf16[1024,1024]{1,0:T(8,128)(2,1)} fusion(bf16[1000,1024]{1,0:T(8,128)(2,1)S(1)} %multiply_convert_fusion, s32[1024]{0:T(1024)S(1)} %broadcast_subtract_fusion), kind=kOutput, calls=%fused_computation.11 | convolution fusion | flops 2099224576 | bytes 4149248 | tf_op jit(solution)/shard_map/dot_general | solution.py:398
  130.2 0.0 all-reduce.2.cloned.1.call-update
  130.2 0.0 reduce-scatter.4.cloned.1.call-start
  130.2 32.5 %all-gather.2.cloned.1.call-done = bf16[2,256,5120]{2,1,0:T(8,128)(2,1)} async-done(((bf16[2,256,640]{2,1,0:T(8,128)(2,1)}), bf16[2,256,5120]{2,1,0:T(8,128)(2,1)}) %all-gather.2.cloned.1.call-update) | async-done | bytes 5242896 | tf_op jit(solution)/shard_map/all_gather | solution.py:393
  162.8 7.9 %fusion.5 = bf16[256,1024]{1,0:T(8,128)(2,1)S(1)} fusion(bf16[1024,5120]{1,0:T(8,128)(2,1)} %refs_2_.1, bf16[2,256,5120]{2,1,0:T(8,128)(2,1)} %all-gather.2.cloned.1.call-done), kind=kOutput, calls=%fused_computation.12 | convolution fusion | flops 2684616704 | bytes 13631488 | tf_op jit(solution)/shard_map/dot_general | solution.py:340
  170.6 0.0 copy-done.7
  170.6 0.0 copy-start.4
  170.7 7.4 %fusion.6 = bf16[256,1024]{1,0:T(8,128)(2,1)S(1)} fusion(bf16[1024,5120]{1,0:T(8,128)(2,1)} %refs_2_.1, bf16[2,256,5120]{2,1,0:T(8,128)(2,1)S(1)} %copy-done.7), kind=kOutput, calls=%fused_computation.13 | convolution fusion | flops 2684616704 | bytes 13631488 | tf_op jit(solution)/shard_map/dot_general | solution.py:340
  178.1 0.0 copy-start.2
  178.1 112.0 %all-reduce.2.cloned.1.call-done = bf16[1024,1024]{1,0:T(8,128)(2,1)} async-done(((bf16[1024,1024]{1,0:T(8,128)(2,1)}), bf16[1024,1024]{1,0:T(8,128)(2,1)}) %all-reduce.2.cloned.1.call-update) | async-done | bytes 2097168 | tf_op jit(solution)/shard_map/psum | solution.py:399
  290.0 2.5 convolution_convert_fusion
  292.5 0.0 copy-done.4
  292.5 0.0 copy-done.2
  292.6 0.0 copy-done
  292.6 0.7 convolution_convert_fusion.1
  293.3 0.1 pad_maximum_fusion
  293.4 1.3 copy.25
  294.7 0.0 reduce-scatter.4.cloned.1.call-update
  294.8 0.3 multiply_cosine_fusion
  295.1 0.5 multiply_reduce_fusion
  295.6 18.8 %psum.23 = f32[1024]{0:T(1024)S(1)} all-reduce(f32[1024]{0:T(1024)S(1)} %multiply_reduce_fusion), channel_id=1, replica_groups=mesh['dp'=8,'tensor'=16] {'dp'}, use_global_device_ids=true, to_apply=%region_6.0 | all-reduce | flops 1024 | bytes 8192 | tf_op jit(solution)/shard_map/psum | solution.py:405
  314.4 0.1 add_rsqrt_fusion
  314.5 0.0 copy-done.5
  314.5 1.0 copy.23
  315.5 0.0 copy-done.3
  315.5 1.0 copy.24
  316.5 18.6 %reduce-scatter.4.cloned.1.call-done = bf16[128,512]{1,0:T(8,128)(2,1)} async-done(((bf16[1024,512]{1,0:T(8,128)(2,1)}), bf16[128,512]{1,0:T(8,128)(2,1)}) %reduce-scatter.4.cloned.1.call-update) | async-done | bytes 131088
  335.1 1.0 copy.26
  336.2 0.1 copy.30
  336.3 0.1 copy.29
  336.4 0.1 copy.27
  336.5 0.1 copy.28
  336.6 0.1 subtract_convert_fusion
  336.7 0.3 fusion.7
  337.0 0.6 subtract_bitcast_fusion
  (14 shorter events, 0.1 us)
Async XLA Ops:
  8.0 154.8 %all-gather.2.cloned.1.call-start = ((), (), s32[]{:S(2)}) async-start(), calls=%async_computation.1 | async-start | bytes 5898240 | tf_op jit(solution)/shard_map/all_gather | solution.py:393
  98.0 192.1 %all-reduce.2.cloned.1.call-start = ((), (), s32[]{:S(2)}) async-start(), calls=%async_computation.2 | async-start | bytes 4194304 | tf_op jit(solution)/shard_map/psum | solution.py:399
  98.0 24.5 %copy-start.6 = (s32[1024]{0:T(1024)S(1)}, s32[1024]{0:T(1024)}, u32[]{:S(2)}) copy-start(s32[1024]{0:T(1024)} %param.7) | copy-start | bytes 12292
  125.1 1.3 copy-start.1
  130.2 204.9 %reduce-scatter.4.cloned.1.call-start = ((), (), s32[]{:S(2)}) async-start(), calls=%async_computation.3 | async-start | bytes 1179648
  162.8 7.9 %copy-start.7 = (bf16[2,256,5120]{2,1,0:T(8,128)(2,1)S(1)}, bf16[2,256,5120]{2,1,0:T(8,128)(2,1)}, u32[]{:S(2)}) copy-start(bf16[2,256,5120]{2,1,0:T(8,128)(2,1)} %all-gather.2.cloned.1.call-done) | copy-start | bytes 15728644
  170.6 121.9 %copy-start.4 = (bf16[256,1024]{1,0:T(8,128)(2,1)}, bf16[256,1024]{1,0:T(8,128)(2,1)S(1)}, u32[]{:S(2)}) copy-start(bf16[256,1024]{1,0:T(8,128)(2,1)S(1)} %fusion.5) | copy-start | bytes 1572868
  178.1 114.5 %copy-start.2 = (bf16[256,1024]{1,0:T(8,128)(2,1)}, bf16[256,1024]{1,0:T(8,128)(2,1)S(1)}, u32[]{:S(2)}) copy-start(bf16[256,1024]{1,0:T(8,128)(2,1)S(1)} %fusion.6) | copy-start | bytes 1572868
  290.0 2.5 copy-start
  294.7 19.8 %copy-start.5 = (bf16[256,1024]{1,0:T(8,128)(2,1)S(1)}, bf16[256,1024]{1,0:T(8,128)(2,1)}, u32[]{:S(2)}) copy-start(bf16[256,1024]{1,0:T(8,128)(2,1)} %copy-done.4) | copy-start | bytes 1572868
  294.7 20.8 %copy-start.3 = (bf16[256,1024]{1,0:T(8,128)(2,1)S(1)}, bf16[256,1024]{1,0:T(8,128)(2,1)}, u32[]{:S(2)}) copy-start(bf16[256,1024]{1,0:T(8,128)(2,1)} %copy-done.2) | copy-start | bytes 1572868
Sparse Core Ops, SparseCore 0:
  98.1 64.6 all-gather.1
  294.9 40.1 reduce-scatter.3
Sparse Core Ops, SparseCore 1:
  130.3 159.7 all-reduce.1

commit v2 on v1

--- a/solution.py
+++ b/solution.py
@@ -336,8 +336,427 @@
     )(old_embed, turned, expand_in, query_out, key_out)
 
 
-def contract_last(left_side, right_side):
-    return lax.dot_general(left_side, right_side, LAST, preferred_element_type=jnp.float32)
+class Flow:
+    def __init__(self):
+        self.sends = {}
+        self.tasks = []
+
+    def send(self, name, link, megabytes, source, target, to):
+        assert name not in self.sends
+        self.sends[name] = (link, megabytes, source, target, to)
+        return name
+
+    def task(self, needs, cost, run, sends=(), rank=5, after=(), name=None):
+        self.tasks.append((frozenset(needs), cost, run, tuple(sends), rank, frozenset(after), name))
+
+    def arrange(self, rates):
+        free, landing, done, order = {}, {}, set(), []
+        left = list(range(len(self.tasks)))
+        now = 0.0
+        while left:
+            ready = []
+            for number in left:
+                needs, _, _, _, rank, after, _ = self.tasks[number]
+                if after <= done and all(landing.get(need, 1e9) <= now for need in needs):
+                    ready.append((rank, number))
+            if not ready:
+                later = [
+                    max(landing.get(need, 1e9) for need in self.tasks[number][0])
+                    for number in left
+                    if self.tasks[number][5] <= done and self.tasks[number][0]
+                ]
+                assert later and min(later) < 1e8
+                now = min(later)
+                continue
+            number = min(ready)[1]
+            left.remove(number)
+            order.append(number)
+            _, cost, _, sends, _, _, name = self.tasks[number]
+            now += cost
+            if name is not None:
+                done.add(name)
+            for send in sends:
+                link, megabytes = self.sends[send][:2]
+                free[link] = max(free.get(link, 0.0), now) + megabytes / rates[link]
+                landing[send] = free[link] + 1.5
+        self.length = now
+        return order
+
+    def emit(self, order, send_sem, recv_sem):
+        number_of = {name: number for number, name in enumerate(self.sends)}
+
+        def copy_of(name):
+            _, _, source, target, to = self.sends[name]
+            return pltpu.make_async_remote_copy(
+                src_ref=source(),
+                dst_ref=target(),
+                send_sem=send_sem.at[number_of[name]],
+                recv_sem=recv_sem.at[number_of[name]],
+                device_id=to(),
+                device_id_type=MESH,
+            )
+
+        arrived, started = set(), []
+        for number in order:
+            needs, _, run, sends, _, _, _ = self.tasks[number]
+            for need in sorted(needs - arrived, key=str):
+                copy_of(need).wait_recv()
+                arrived.add(need)
+            if run is not None:
+                run()
+            for send in sends:
+                copy_of(send).start()
+                started.append(send)
+        assert arrived == set(self.sends) and sorted(started, key=str) == sorted(self.sends, key=str)
+        for name in self.sends:
+            copy_of(name).wait_send()
+
+
+LINK_RATES = {
+    "y+": 0.0465, "y-": 0.0465, "z": 0.0465, "x+": 0.0465, "x-": 0.0465, "h": 0.0465, "c": 0.3, "far": 0.03,
+}
+DP_PEERS = ((1, 2), (0, 2), (1, 1), (1, 3), (1, 0), (0, 1), (0, 3))
+PEER_LINKS = {(1, 2): "far", (0, 2): "far", (1, 1): "y+", (1, 3): "y-", (1, 0): "z", (0, 1): "y+", (0, 3): "y-"}
+INNER_MODES = ((True, "y+"), (True, "y-"), (True, "y+"), (False, "y-"))
+
+
+def second_kernel(
+    sizes, raw_ref, x_ref, tokens_ref, inner_ref, e_ref,
+    ge_ref, gq_ref, gk_ref, both_ref,
+    raw_all, x_all, e_all, inner_all, grown_sum, lanes, squares, squares_in, ge_pad,
+    masked, core_in, left_in, right_in, left_block, right_block, half_in, hidden,
+    part_out, part_in, own_part, send_sem, recv_sem, local_sem,
+):
+    place = Place()
+    vocab_rows, new_cols = raw_ref.shape
+    head_cols, slab = inner_ref.shape[1:]
+    token_rows = tokens_ref.shape[0]
+    grown = (gq_ref, gk_ref)
+    old_width, new_width = sizes
+    per_seq = both_ref.shape[0]
+
+    barrier = pltpu.get_barrier_semaphore()
+    friends = [place.across(link) for link in ("x+", "x-", "h", "c")]
+    friends += [(place.dp_at(rel), place.tensor) for rel in DP_PEERS]
+    for friend in friends:
+        pl.semaphore_signal(barrier, inc=1, device_id=friend, device_id_type=MESH)
+    local = [
+        pltpu.make_async_copy(raw_ref, raw_all, local_sem.at[0]),
+        pltpu.make_async_copy(x_ref, x_all, local_sem.at[1]),
+        pltpu.make_async_copy(inner_ref, inner_all.at[place.dp], local_sem.at[2]),
+        pltpu.make_async_copy(e_ref, e_all, local_sem.at[3]),
+    ]
+    for copy in local:
+        copy.start()
+    pl.semaphore_wait(barrier, len(friends))
+
+    flow = Flow()
+
+    half = head_cols // 2
+    sends = []
+    for chunk, (z_first, extra) in enumerate(INNER_MODES):
+        sends += gather_dp("I", chunk, z_first, extra)
+    brought_by = {
+        ("I", seen_by_receiver(link, rel), chunk): (link, rel, chunk) for link, _, rel, chunk in sends
+    }
+
+    def inner_view(ref, chunk):
+        return ref.at[chunk // 2, pl.ds((chunk % 2) * half, half), :]
+
+    first, after = [], {}
+    for link, kind, rel, chunk in sends:
+        def source(rel=rel, chunk=chunk):
+            if not any(rel):
+                return inner_view(inner_ref, chunk)
+            return inner_view(inner_all.at[place.dp_at(rel)], chunk)
+
+        def target(rel=rel, chunk=chunk):
+            return inner_view(inner_all.at[place.dp_at(rel)], chunk)
+
+        name = ("I", link, rel, chunk)
+        flow.send(name, link, half * slab * 2e-6, source, target, lambda link=link: place.across(link))
+        cause = brought_by.get((kind, rel, chunk))
+        if cause is None:
+            first.append(name)
+        else:
+            after.setdefault(("I",) + cause, []).append(name)
+    flow.task((), 0.1, None, first, rank=0)
+    for link, _, rel, chunk in sends:
+        name = ("I", link, rel, chunk)
+        flow.task((name,), 0.02, None, after.get(name, ()), rank=0)
+
+    tile = 256
+    e_rows = e_all.shape[0]
+    seen = set()
+
+    def add_grown(rel, matrix):
+        at = place.dp_at(rel)
+        columns = pl.ds(pl.multiple_of(at * slab, 128), slab)
+        fresh = matrix not in seen
+        seen.add(matrix)
+
+        def body(number, _):
+            rows = pl.ds(pl.multiple_of(number * tile, tile), tile)
+            part = lax.dot_general(
+                e_all[rows, columns], inner_all[at, matrix], LAST, preferred_element_type=jnp.float32
+            )
+            if fresh:
+                grown_sum[matrix, rows, :] = part
+            else:
+                grown_sum[matrix, rows, :] += part
+            return 0
+
+        lax.fori_loop(0, e_rows // tile, body, 0)
+
+    for rel in [(flip, shift) for flip in (0, 1) for shift in (0, 1, 3, 2)]:
+        for matrix in range(2):
+            needs = []
+            if any(rel):
+                for chunk in (2 * matrix, 2 * matrix + 1):
+                    needs.append(("I",) + brought_by[("I", rel, chunk)])
+            flow.task(
+                needs, 0.8, lambda rel=rel, matrix=matrix: add_grown(rel, matrix),
+                rank=6, name=("grown", rel, matrix), after=(("loaded",),),
+            )
+
+    def lane_sums(values_ref):
+        rows, columns = values_ref.shape
+        sums = None
+        for start in range(0, columns, 128):
+            part = jnp.square(values_ref[:, start:start + 128].astype(jnp.float32))
+            sums = part if sums is None else sums + part
+        lanes[pl.ds(lanes.shape[0] - 32, 32), :] = jnp.zeros((32, 128), jnp.float32)
+        lanes[pl.ds(0, rows), :] = sums
+        return jnp.sum(lanes[...].T, axis=0, keepdims=True)
+
+    def load_and_square():
+        for copy in local:
+            copy.wait()
+        row = lax.broadcasted_iota(jnp.int32, squares.shape, 0)
+        new_row = jnp.broadcast_to(lane_sums(raw_all), squares.shape)
+        old_row = jnp.broadcast_to(lane_sums(x_all), squares.shape)
+        squares[...] = jnp.where(row == 0, new_row, jnp.where(row == 1, old_row, 0.0))
+
+    square_sends = []
+    for number, rel in enumerate(DP_PEERS):
+        square_sends.append(
+            flow.send(
+                ("S", number), "far", 0.03, lambda: squares, lambda number=number: squares_in.at[number],
+                lambda rel=rel: (place.dp_at(rel), place.tensor),
+            )
+        )
+    flow.task((), 4.0, load_and_square, square_sends, rank=1, name=("loaded",))
+
+    def rescale():
+        total = squares[...]
+        for number in range(len(DP_PEERS)):
+            total = total + squares_in[number]
+        factor = jnp.sqrt(
+            (total[1:2] / old_width + EMBED_EPSILON) / (total[0:1] / new_width + EMBED_EPSILON)
+        )
+        column = jnp.broadcast_to(factor, (128, factor.shape[1])).T[:vocab_rows]
+        ge_pad[pl.ds(ge_pad.shape[0] - 32, 32), :] = jnp.zeros((32, new_cols), jnp.bfloat16)
+        for start in range(0, new_cols, 128):
+            scaled = (raw_all[:, start:start + 128] * column).astype(jnp.bfloat16)
+            ge_pad[pl.ds(0, vocab_rows), start:start + 128] = scaled
+            ge_ref[:, start:start + 128] = scaled
+
+    flow.task(square_sends, 2.5, rescale, rank=1, name=("scaled",), after=(("loaded",),))
+
+    core_rows, chip_rows, own_rows = token_rows // 2, token_rows // 8, token_rows // 16
+    mine = place.core * core_rows
+    theirs = (1 - place.core) * core_rows
+    middle = new_cols // 2
+
+    def rows_of(core, shift):
+        start = (1 - place.core if core else place.core) * core_rows + ((place.x + shift + 4) % 4) * chip_rows
+        return pl.ds(pl.multiple_of(start, chip_rows), chip_rows)
+
+    def small_rows(flip):
+        z_hi = 1 - place.z_hi if flip else place.z_hi
+        start = mine + place.x * chip_rows + z_hi * own_rows
+        return pl.ds(pl.multiple_of(start, own_rows), own_rows)
+
+    def choose(start):
+        def body(number, _):
+            rows = pl.ds(pl.multiple_of(start + number * tile, tile), tile)
+            ids = tokens_ref[rows, :] - place.tensor * vocab_rows
+            column = lax.broadcasted_iota(jnp.int32, (tile, ge_pad.shape[0]), 1)
+            chosen = jnp.where(ids == column, 1.0, 0.0).astype(jnp.bfloat16)
+            masked[rows, :] = jnp.dot(
+                chosen, ge_pad[...], preferred_element_type=jnp.float32
+            ).astype(jnp.bfloat16)
+            return 0
+
+        lax.fori_loop(0, core_rows // tile, body, 0)
+
+    core_mb = core_rows * new_cols * 2e-6
+    to = lambda link: (lambda: place.across(link))
+    whole = lambda start, size: pl.ds(pl.multiple_of(start, size), size)
+    flow.send("c1", "c", core_mb, lambda: masked.at[whole(theirs, core_rows), :], lambda: core_in, to("c"))
+    flow.task((), 1.5, lambda: choose(theirs), ("c1",), rank=1, name=("theirs",), after=(("scaled",),))
+    flow.task((), 1.5, lambda: choose(mine), rank=1, name=("mine",), after=(("theirs",),))
+
+    def add_core():
+        rows = whole(mine, core_rows)
+        masked[rows, :] += core_in[...]
+
+    block_mb = core_mb / 4
+    left_part, right_part = pl.ds(0, middle), pl.ds(middle, middle)
+    flow.send("r+", "x+", block_mb / 2, lambda: masked.at[rows_of(0, 2), left_part], lambda: left_in, to("x+"))
+    flow.send("r-", "x-", block_mb / 2, lambda: masked.at[rows_of(0, 2), right_part], lambda: right_in, to("x-"))
+    flow.task(("c1",), 0.7, add_core, ("r+", "r-"), rank=1, name=("core",), after=(("mine",),))
+
+    def add_left():
+        masked[rows_of(0, 1), left_part] += left_in[...]
+
+    def add_right():
+        masked[rows_of(0, 3), right_part] += right_in[...]
+
+    flow.send("b+", "x+", block_mb, lambda: masked.at[rows_of(0, 1), :], lambda: left_block, to("x+"))
+    flow.send("b-", "x-", block_mb, lambda: masked.at[rows_of(0, 3), :], lambda: right_block, to("x-"))
+    flow.task(("r+",), 0.1, add_left, ("b+",), rank=1, after=(("core",),))
+    flow.task(("r-",), 0.1, add_right, ("b-",), rank=1, after=(("core",),))
+
+    def add_blocks():
+        masked[rows_of(0, 0), :] += left_block[...] + right_block[...]
+
+    flow.send("h1", "h", block_mb / 2, lambda: masked.at[small_rows(1), :], lambda: half_in, to("h"))
+    flow.task(("b+", "b-"), 0.2, add_blocks, ("h1",), rank=1, name=("blocks",), after=(("core",),))
+
+    def add_half():
+        hidden[small_rows(0), :] = masked[small_rows(0), :] + half_in[...]
+
+    flow.send("h2", "h", block_mb / 2, lambda: hidden.at[small_rows(0), :], lambda: hidden.at[small_rows(0), :], to("h"))
+    flow.task(("h1",), 0.1, add_half, ("h2",), rank=1, name=("half",), after=(("blocks",),))
+
+    def same(name, link, megabytes, view):
+        return flow.send(name, link, megabytes, lambda: hidden.at[view()], lambda: hidden.at[view()], to(link))
+
+    every = pl.ds(0, new_cols)
+    same("a+", "x+", block_mb, lambda: (rows_of(0, 0), every))
+    same("a-", "x-", block_mb, lambda: (rows_of(0, 0), every))
+    same("f+", "x+", block_mb / 2, lambda: (rows_of(0, 3), left_part))
+    same("f-", "x-", block_mb / 2, lambda: (rows_of(0, 1), right_part))
+    for shift in range(4):
+        same(("c", shift), "c", block_mb, lambda shift=shift: (rows_of(0, shift), every))
+    flow.task(("h2",), 0.02, None, ("a+", "a-", ("c", 0)), rank=0, after=(("half",),))
+    flow.task(("a+",), 0.02, None, ("f+", ("c", 3)), rank=0)
+    flow.task(("a-",), 0.02, None, ("f-", ("c", 1)), rank=0)
+    flow.task(("f+", "f-"), 0.02, None, (("c", 2),), rank=0)
+
+    def finish_grown():
+        for matrix in range(2):
+            grown[matrix][...] = grown_sum[matrix].astype(jnp.bfloat16)
+
+    flow.task(
+        (), 1.0, finish_grown, rank=7, name=("grown",),
+        after=[("grown", (flip, shift), matrix) for flip in (0, 1) for shift in range(4) for matrix in (0, 1)],
+    )
+
+    def partials(rel):
+        rows = pl.ds(pl.multiple_of(place.dp_at(rel) * per_seq, per_seq), per_seq)
+        block = hidden[rows, :]
+        values = [jnp.dot(block, grown[matrix][...], preferred_element_type=jnp.float32) for matrix in range(2)]
+        sums = None
+        for start in range(0, new_cols, 128):
+            part = jnp.square(block[:, start:start + 128].astype(jnp.float32))
+            sums = part if sums is None else sums + part
+        return values + [sums]
+
+    def put_partials(number, rel):
+        start = 0
+        for value in partials(rel):
+            part_out[number, :, start:start + value.shape[1]] = value.astype(jnp.bfloat16)
+            start += value.shape[1]
+
+    needs = ["h2", "a+", "a-", "f+", "f-"] + [("c", shift) for shift in range(4)]
+    width = part_out.shape[2]
+    names = []
+    for number, rel in enumerate(DP_PEERS):
+        name = flow.send(
+            ("P", number), PEER_LINKS[rel], per_seq * width * 2e-6,
+            lambda number=number: part_out.at[number], lambda number=number: part_in.at[number],
+            lambda rel=rel: (place.dp_at(rel), place.tensor),
+        )
+        names.append(name)
+        flow.task(
+            needs, 0.5, lambda number=number, rel=rel: put_partials(number, rel), (name,),
+            rank=8, after=(("grown",), ("half",)), name=name,
+        )
+
+    def keep_own():
+        start = 0
+        for value in partials((0, 0)):
+            own_part[:, start:start + value.shape[1]] = value
+            start += value.shape[1]
+
+    flow.task(needs, 0.5, keep_own, rank=9, name=("own",), after=names)
+
+    def add_up():
+        total = own_part[...]
+        for number in range(len(DP_PEERS)):
+            total = total + part_in[number].astype(jnp.float32)
+        square_sum = jnp.sum(total[:, 2 * head_cols:], axis=1, keepdims=True)
+        both_ref[...] = total[:, :2 * head_cols] * lax.rsqrt(square_sum / new_width + TOKEN_EPSILON)
+
+    flow.task(names, 1.0, add_up, rank=9, after=(("own",),))
+    flow.emit(flow.arrange(LINK_RATES), send_sem, recv_sem)
+
+
+def exchange_and_check(raw_rows, old_embed, token_ids, inner, expand_in):
+    vocab_rows, new_cols = raw_rows.shape
+    slab = old_embed.shape[1]
+    head_cols = inner.shape[1]
+    tokens = token_ids.shape[0]
+    padded = -(-vocab_rows // 128) * 128
+    per_seq = tokens // N_DP
+    width = 2 * head_cols + 128
+    anywhere = pl.BlockSpec(memory_space=pl.ANY)
+    inside = pl.BlockSpec(memory_space=pltpu.VMEM)
+    bf16, f32 = jnp.bfloat16, jnp.float32
+    count = 7 * len(INNER_MODES) + 7 + 1 + 4 + 2 + 4 + 4 + 7
+    sizes = (expand_in.shape[1], D_NEW)
+    return pl.pallas_call(
+        lambda *refs: second_kernel(sizes, *refs),
+        out_shape=(
+            jax.ShapeDtypeStruct((vocab_rows, new_cols), bf16),
+            jax.ShapeDtypeStruct((new_cols, head_cols), bf16),
+            jax.ShapeDtypeStruct((new_cols, head_cols), bf16),
+            jax.ShapeDtypeStruct((per_seq, 2 * head_cols), f32),
+        ),
+        in_specs=[anywhere, anywhere, inside, anywhere, anywhere],
+        out_specs=(inside,) * 4,
+        scratch_shapes=[
+            pltpu.VMEM((vocab_rows, new_cols), f32),
+            pltpu.VMEM((vocab_rows, slab), bf16),
+            pltpu.VMEM(expand_in.shape, bf16),
+            pltpu.VMEM((N_DP,) + inner.shape, bf16),
+            pltpu.VMEM((2, new_cols, head_cols), f32),
+            pltpu.VMEM((padded, 128), f32),
+            pltpu.VMEM((8, padded), f32),
+            pltpu.VMEM((7, 8, padded), f32),
+            pltpu.VMEM((padded, new_cols), bf16),
+            pltpu.VMEM((tokens, new_cols), bf16),
+            pltpu.VMEM((tokens // 2, new_cols), bf16),
+            pltpu.VMEM((tokens // 8, new_cols // 2), bf16),
+            pltpu.VMEM((tokens // 8, new_cols // 2), bf16),
+            pltpu.VMEM((tokens // 8, new_cols), bf16),
+            pltpu.VMEM((tokens // 8, new_cols), bf16),
+            pltpu.VMEM((tokens // 16, new_cols), bf16),
+            pltpu.VMEM((tokens, new_cols), bf16),
+            pltpu.VMEM((7, per_seq, width), bf16),
+            pltpu.VMEM((7, per_seq, width), bf16),
+            pltpu.VMEM((per_seq, width), f32),
+            pltpu.SemaphoreType.DMA((count,)),
+            pltpu.SemaphoreType.DMA((count,)),
+            pltpu.SemaphoreType.DMA((4,)),
+        ],
+        compiler_params=pltpu.CompilerParams(
+            collective_id=2, has_side_effects=True, vmem_limit_bytes=VMEM_LIMIT
+        ),
+        name="exchange_and_check",
+    )(raw_rows, old_embed, token_ids.reshape(tokens, 1), inner, expand_in)
 
 
 def rotate(values, head_count):
@@ -374,41 +793,12 @@
 
 
 def on_device(token_ids, old_embed, expand_in, query_out, key_out, old_query, old_key):
-    vocab_rows = old_embed.shape[0]
-    old_width = expand_in.shape[1]
     head_cols = query_out.shape[0]
-    head_count = head_cols // HEAD
     raw_rows, inner = gather_and_grow(old_embed, expand_in, query_out, key_out, old_query, old_key)
-    squares = jnp.stack(
-        [
-            jnp.sum(jnp.square(old_embed.astype(jnp.float32)), axis=1),
-            jnp.sum(jnp.square(raw_rows), axis=1),
-        ]
+    grown_embedding, grown_query, grown_key, both = exchange_and_check(
+        raw_rows, old_embed, token_ids, inner, expand_in
     )
-    squares = lax.psum(squares, "dp")
-    factor = jnp.sqrt(
-        (squares[0] / old_width + EMBED_EPSILON) / (squares[1] / D_NEW + EMBED_EPSILON)
-    )
-    grown_embedding = (raw_rows * factor[:, None]).astype(jnp.bfloat16)
-    inner = lax.all_gather(inner, "dp", axis=2, tiled=True)
-    grown_query = contract_last(expand_in, inner[0]).astype(jnp.bfloat16)
-    grown_key = contract_last(expand_in, inner[1]).astype(jnp.bfloat16)
-    offset_ids = token_ids - lax.axis_index("tensor") * vocab_rows
-    chosen = (offset_ids[:, None] == jnp.arange(vocab_rows)[None, :]).astype(jnp.bfloat16)
-    partial_rows = jnp.dot(chosen, grown_embedding, preferred_element_type=jnp.float32)
-    hidden_cols = lax.psum(partial_rows.astype(jnp.bfloat16), "tensor")
-    square_sum = jnp.sum(jnp.square(hidden_cols.astype(jnp.float32)), axis=1)
-    queries = jnp.dot(hidden_cols, grown_query, preferred_element_type=jnp.float32)
-    key_proj = jnp.dot(hidden_cols, grown_key, preferred_element_type=jnp.float32)
-    both = jnp.concatenate([queries, key_proj], axis=1).astype(jnp.bfloat16)
-    both = lax.psum_scatter(both, "dp", scatter_dimension=0, tiled=True).astype(jnp.float32)
-    square_sum = lax.psum(square_sum, "dp")
-    square_sum = lax.dynamic_slice(
-        square_sum, (lax.axis_index("dp") * both.shape[0],), (both.shape[0],)
-    )
-    inverse_rms = lax.rsqrt(square_sum / D_NEW + TOKEN_EPSILON)
-    both = both * inverse_rms[:, None]
-    attention_entropy = entropy_of(both[:, :head_cols], both[:, head_cols:], head_count)
+    attention_entropy = entropy_of(both[:, :head_cols], both[:, head_cols:], head_cols // HEAD)
     return (grown_embedding, grown_query, grown_key, attention_entropy)
 
 

time: 345 us -> 186 us (0.54)
  waiting for transfers between devices: 163 us -> 0 us
  Pallas kernels: 87.8 us -> 175 us
  blocking collectives: 39.1 us -> 0 us
  matrix products: 22.5 us -> 0.27 us
  between operations: 15.8 us -> 0.74 us
  other arithmetic: 10.4 us -> 3.08 us
    psum x1 -> x0, waiting for transfers between devices: 112 us -> none  [on_device(): hidden_cols = lax.psum(partial_rows.astype(jnp.bfloat16), 'tensor')]
    pallas_call x0 -> x1, Pallas kernels: none -> 87.2 us  [exchange_and_check(): pl.pallas_call(lambda *refs: second_kernel(sizes, *refs), out_shape=(jax....]
    psum x2 -> x0, blocking collectives: 39.1 us -> none  [the longest x1 20.3 us: on_device(): squares = lax.psum(squares, 'dp')]
    all_gather x1 -> x0, waiting for transfers between devices: 32.5 us -> none  [on_device(): inner = lax.all_gather(inner, 'dp', axis=2, tiled=True)]
    dot_general x5 -> x0, matrix products: 22.3 us -> none  [the longest x2 15.3 us: contract_last(): lax.dot_general(left_side, right_side, LAST, preferred_element_type=jnp.f...]
    unnamed x4 -> x0, waiting for transfers between devices: 18.7 us -> none
    reduce_sum x3 -> x0, other arithmetic: 4.6 us -> none  [the longest x1 2.5 us: on_device(): jnp.sum(jnp.square(raw_rows), axis=1)]
  transfers between devices with their start and end apart: 3 -> 0, of which waited for: 3 -> 0; matrix products, arithmetic and copies ran while one was open for 8% -> 0% of each run, Pallas kernels for 0% -> 0%
where the time goes in v2:
time: 186 us; the launch traced here: 185 us
  Pallas kernels  175 us (94%)
  local copies, waits for them, and re-layouts  5.54 us (3%)
  other arithmetic  3.08 us (2%)
    pallas_call x1, Pallas kernels, gather_and_grow(): pl.pallas_call(lambda *refs: first_kernel(plan, cuts, *refs), out_shape=(...  87.7 us
    pallas_call x1, Pallas kernels, exchange_and_check(): pl.pallas_call(lambda *refs: second_kernel(sizes, *refs), out_shape=(jax....  87.2 us

profile of v2, /device:TPU:0, one launch (start us, length us, event | category | flops | bytes accessed | tf_op | source)
XLA Modules:
  0.0 184.5 jit_solution(18379252123648029859)
XLA Ops:
  0.6 2.1 %pad_maximum_fusion.refs_1_ = bf16[2,320,640]{2,1,0:T(8,128)(2,1)} fusion(bf16[1,320,640]{2,1,0:T(8,128)(2,1)} %bitcast.9, bf16[1,320,640]{2,1,0:T(8,128)(2,1)} %bitcast.10), kind=kLoop, calls=%fused_computation.1 | loop fusion | flops 409600 | bytes 1638400 | tf_op jit(solution)/shard_map/stack | solution.py:309
  2.7 0.0 copy-start.3
  2.7 87.7 %gather_and_grow.1 = (f32[1000,1024]{1,0:T(8,128)}, bf16[2,256,640]{2,1,0:T(8,128)(2,1)}) custom-call(bf16[1000,640]{1,0:T(8,128)(2,1)} %refs_1_.1, bf16[2,320,640]{2,1,0:T(8,128)(2,1)} %pad_maximum_fusion.refs_1_, bf16[1024,5120]{1,0:T(8,128)(2,1)} %refs_4_.3, bf16[256,5120]{1,0:T(8,128)(2,1)} %refs_3_.1, bf16[256,5120]{1,0:T(8,128)(2,1)} %refs_4_.2), custom_call_target="tpu_custom_call" | custom-call | tf_op jit(solution)/shard_map/gather_and_grow/pallas_call | solution.py:314
  90.5 0.0 copy-done.3
  90.5 1.0 copy.15.refs_2_
  91.5 87.2 %exchange_and_check.1 = (bf16[1000,1024]{1,0:T(8,128)(2,1)}, bf16[1024,256]{1,0:T(8,128)(2,1)}, bf16[1024,256]{1,0:T(8,128)(2,1)}, f32[128,512]{1,0:T(8,128)}) custom-call(f32[1000,1024]{1,0:T(8,128)} %get-tuple-element.10.refs_0_, bf16[1000,640]{1,0:T(8,128)(2,1)} %refs_1_.1, s32[1024,1]{1,0:T(8,128)} %copy.15.refs_2_, ...), custom_call_target="tpu_custom_call" | custom-call | tf_op jit(solution)/shard_map/exchange_and_check/pallas_call | solution.py:720
  178.7 0.0 copy-start
  178.7 1.1 fusion.8
  179.8 0.1 reshape.87
  179.9 0.1 reshape.88
  180.0 0.3 fusion.9
  180.3 0.3 multiply_cosine_fusion
  180.7 0.0 copy-start.2
  180.7 0.1 subtract_convert_fusion
  180.8 0.3 fusion
  181.1 0.0 copy-start.1
  181.1 0.6 subtract_bitcast_fusion
  181.6 0.0 copy-done
  181.6 1.3 copy.35
  182.9 0.0 copy-done.2
  182.9 0.8 copy.36
  183.7 0.0 copy-done.1
  183.7 0.8 copy.37
  (3 shorter events, 0.0 us)
Async XLA Ops:
  2.7 87.7 %copy-start.3 = (s32[1024]{0:T(1024)S(1)}, s32[1024]{0:T(1024)}, u32[]{:S(2)}) copy-start(s32[1024]{0:T(1024)} %param.7) | copy-start | bytes 12292
  178.7 3.0 %copy-start = (bf16[1000,1024]{1,0:T(8,128)(2,1)S(1)}, bf16[1000,1024]{1,0:T(8,128)(2,1)}, u32[]{:S(2)}) copy-start(bf16[1000,1024]{1,0:T(8,128)(2,1)} %get-tuple-element.38) | copy-start | bytes 6144004
  180.7 2.3 %copy-start.2 = (bf16[1024,256]{1,0:T(8,128)(2,1)S(1)}, bf16[1024,256]{1,0:T(8,128)(2,1)}, u32[]{:S(2)}) copy-start(bf16[1024,256]{1,0:T(8,128)(2,1)} %get-tuple-element.39) | copy-start | bytes 1572868
  181.1 2.7 %copy-start.1 = (bf16[1024,256]{1,0:T(8,128)(2,1)S(1)}, bf16[1024,256]{1,0:T(8,128)(2,1)}, u32[]{:S(2)}) copy-start(bf16[1024,256]{1,0:T(8,128)(2,1)} %get-tuple-element.40) | copy-start | bytes 1572868

commit v3 on v0

v3 whole, which is shorter than its diff:
```python
import heapq
import math

import jax
import jax.numpy as jnp
from jax import lax
from jax.experimental import pallas as pl
from jax.experimental.pallas import tpu as pltpu
from jax.sharding import PartitionSpec as P

D_NEW = 8192
HEAD = 128
N_DP = 8
N_TENSOR = 16

EMBED_EPSILON = 1e-06
TOKEN_EPSILON = 1e-05

MESH = pl.DeviceIdType.MESH
LAST = (((1,), (1,)), ((), ()))
VMEM_LIMIT = 67_000_000

STEP = {"y+": 1, "y-": -1, "x+": 1, "x-": -1}


class Place:
    def __init__(self):
        self.dp = lax.axis_index("dp")
        self.tensor = lax.axis_index("tensor")
        self.z_lo = self.dp // 4
        self.y = self.dp % 4
        self.x = self.tensor // 4
        self.z_hi = (self.tensor // 2) % 2
        self.core = self.tensor % 2

    def dp_at(self, rel):
        flip, shift = rel
        z_lo = 1 - self.z_lo if flip else self.z_lo
        return z_lo * 4 + (self.y + shift + 4) % 4

    def tensor_at(self, rel):
        flip, shift, core_flip = rel
        z_hi = 1 - self.z_hi if flip else self.z_hi
        core = 1 - self.core if core_flip else self.core
        return (((self.x + shift + 4) % 4) * 2 + z_hi) * 2 + core

    def across(self, link):
        if link in ("y+", "y-"):
            return (self.dp_at((0, STEP[link])), self.tensor)
        if link == "z":
            return (self.dp_at((1, 0)), self.tensor)
        if link in ("x+", "x-"):
            return (self.dp, self.tensor_at((0, STEP[link], 0)))
        if link == "h":
            return (self.dp, self.tensor_at((1, 0, 0)))
        return (self.dp, self.tensor_at((0, 0, 1)))


def seen_by_receiver(link, rel):
    if link in ("y+", "y-"):
        return (rel[0], (rel[1] - STEP[link]) % 4)
    if link == "z":
        return (1 - rel[0], rel[1])
    if link in ("x+", "x-"):
        return (rel[0], (rel[1] - STEP[link]) % 4, rel[2])
    if link == "h":
        return (1 - rel[0], rel[1], rel[2])
    return (rel[0], rel[1], 1 - rel[2])


def ring_tree(plus, minus, kind, rel, chunk, extra):
    near = (rel[0], (rel[1] - STEP[extra]) % 4) + tuple(rel[2:])
    return [(plus, kind, rel, chunk), (minus, kind, rel, chunk), (extra, kind, near, chunk)]


def gather_dp(kind, chunk, z_first, extra):
    other = "y-" if extra == "y+" else "y+"
    if z_first:
        sends = [("z", kind, (0, 0), chunk)]
        sends += ring_tree("y+", "y-", kind, (0, 0), chunk, extra)
        sends += ring_tree("y+", "y-", kind, (1, 0), chunk, other)
        return sends
    sends = ring_tree("y+", "y-", kind, (0, 0), chunk, extra)
    return sends + [("z", kind, (0, shift), chunk) for shift in (0, 1, 3, 2)]


def gather_tensor(kind, chunk, extra):
    other = "x-" if extra == "x+" else "x+"
    sends = [("h", kind, (0, 0, 0), chunk)]
    sends += ring_tree("x+", "x-", kind, (0, 0, 0), chunk, extra)
    sends += ring_tree("x+", "x-", kind, (1, 0, 0), chunk, other)
    sends += [("c", kind, (flip, shift, 0), chunk) for flip in (0, 1) for shift in (0, 1, 3, 2)]
    return sends


def row_cuts(rows, pieces):
    step = -(-rows // (16 * pieces)) * 16
    return [(start, min(step, rows - start)) for start in range(0, rows, step)]


class Flow:
    def __init__(self):
        self.sends = {}
        self.tasks = []
        self.left_already = set()

    def send(self, name, link, priority, megabytes, source, target, to):
        assert name not in self.sends
        self.sends[name] = (link, priority, megabytes, source, target, to)
        return name

    def task(self, needs, cost, run, sends=(), rank=5, after=(), name=None):
        self.tasks.append((frozenset(needs), cost, run, tuple(sends), rank, frozenset(after), name))

    def arrange(self):
        free, flying, queues = {}, {}, {}
        landed, done, order, heap = set(), set(), [], []
        left = list(range(len(self.tasks)))
        now, serial = 0.0, 0

        def pump(link):
            while queues.get(link) and flying.get(link, 0) < DEPTH.get(link, 1000):
                name = heapq.heappop(queues[link])[2]
                flying[link] = flying.get(link, 0) + 1
                free[link] = max(free.get(link, 0.0), now) + self.sends[name][2] / LINK_RATES[link]
                heapq.heappush(heap, (free[link] + 1.5, len(order), name))
                order.append(("start", name))

        while left or heap:
            if heap and heap[0][0] <= now:
                name = heapq.heappop(heap)[2]
                link = self.sends[name][0]
                landed.add(name)
                flying[link] -= 1
                order.append(("arrive", name))
                now += 0.03
                for number in list(left):
                    needs, cost, run, sends, rank, after, _ = self.tasks[number]
                    if rank == 0 and name in needs and needs <= landed and after <= done:
                        left.remove(number)
                        for send in sends:
                            serial += 1
                            put = (self.sends[send][1], serial, send)
                            heapq.heappush(queues.setdefault(self.sends[send][0], []), put)
                for other in sorted(queues):
                    pump(other)
                continue
            ready = []
            for number in left:
                needs, _, _, _, rank, after, _ = self.tasks[number]
                if after <= done and needs <= landed:
                    ready.append((rank, number))
            if not ready:
                assert heap
                now = max(now, heap[0][0])
                continue
            number = min(ready)[1]
            left.remove(number)
            order.append(("run", number))
            _, cost, _, sends, _, _, name = self.tasks[number]
            now += cost
            if name is not None:
                done.add(name)
            for send in sends:
                serial += 1
                put = (self.sends[send][1], serial, send)
                heapq.heappush(queues.setdefault(self.sends[send][0], []), put)
            for other in sorted(queues):
                pump(other)
        self.length = now
        assert not any(queues.values())
        return order

    def copy_of(self, name):
        _, _, _, source, target, to = self.sends[name]
        number = self.number_of[name]
        return pltpu.make_async_remote_copy(
            src_ref=source(),
            dst_ref=target(),
            send_sem=self.send_sem.at[number],
            recv_sem=self.recv_sem.at[number],
            device_id=to(),
            device_id_type=MESH,
        )

    def wait_left(self, names):
        for name in names:
            if name not in self.left_already:
                self.left_already.add(name)
                self.copy_of(name).wait_send()

    def emit(self, order, send_sem, recv_sem):
        self.number_of = {name: number for number, name in enumerate(self.sends)}
        self.send_sem, self.recv_sem = send_sem, recv_sem
        arrived, started = set(), set()
        for what, which in order:
            if what == "arrive":
                self.copy_of(which).wait_recv()
                arrived.add(which)
            elif what == "start":
                self.copy_of(which).start()
                started.add(which)
            elif self.tasks[which][2] is not None:
                self.tasks[which][2]()
        assert arrived == set(self.sends) and started == set(self.sends)
        self.wait_left(list(self.sends))


DEPTH = {"y+": 3, "y-": 3, "z": 3, "x+": 3, "x-": 3, "h": 3}
LINK_RATES = {
    "y+": 0.0465, "y-": 0.0465, "z": 0.0465, "x+": 0.0465, "x-": 0.0465, "h": 0.0465, "c": 0.3, "far": 0.03,
}
DP_PEERS = ((1, 2), (0, 2), (1, 1), (1, 3), (1, 0), (0, 1), (0, 3))
X_CUTS = 7
X_MODES = ((False, "y+"), (False, "y-"), (True, "y+"), (True, "y-"), (True, "y+"), (True, "y-"), (True, "y+"))
INNER_MODES = ((True, "y+"), (False, "y-"), (True, "y-"), (False, "y+"))
RELS = [(flip, shift) for flip in (0, 1) for shift in (0, 1, 3, 2)]
TILE = 256


def slot_of(rel):
    return rel[0] * 4 + rel[1] - 1


def aligned(start, size):
    return pl.ds(pl.multiple_of(start, size), size)


def whole_kernel(
    sizes, x_ref, w_ref, e_ref, q_ref, k_ref, tokens_ref,
    ge_ref, gq_ref, gk_ref, both_ref,
    x_pad, x_all, raw, w_all, e_all, o_all, total, inner_own, inner_all, grown_sum,
    lanes, squares, squares_in,
    masked, core_in, left_in, right_in, left_block, right_block, half_in, chosen_all, chosen_sum, hidden,
    q_out, q_in, k_out, k_in, own_part,
    send_sem, recv_sem, local_sem,
):
    place = Place()
    vocab_rows, slab = x_ref.shape
    new_cols, old_width = e_ref.shape
    new_width = sizes
    head_cols = q_ref.shape[0]
    token_rows = tokens_ref.shape[0]
    out_slab, in_slab = w_ref.shape[1:]
    grown = (gq_ref, gk_ref)
    per_seq = both_ref.shape[0]
    cuts = row_cuts(vocab_rows, X_CUTS)
    assert len(cuts) == X_CUTS

    barrier = pltpu.get_barrier_semaphore()
    friends = [place.across(link) for link in ("x+", "x-", "h", "c")]
    friends += [(place.dp_at(rel), place.tensor) for rel in DP_PEERS]
    for friend in friends:
        pl.semaphore_signal(barrier, inc=1, device_id=friend, device_id_type=MESH)
    local = [
        pltpu.make_async_copy(x_ref, x_pad.at[pl.ds(0, vocab_rows), :], local_sem.at[0]),
        pltpu.make_async_copy(w_ref.at[0], w_all.at[0, place.tensor], local_sem.at[1]),
        pltpu.make_async_copy(w_ref.at[1], w_all.at[1, place.tensor], local_sem.at[2]),
        pltpu.make_async_copy(q_ref, o_all.at[0], local_sem.at[3]),
        pltpu.make_async_copy(e_ref, e_all, local_sem.at[4]),
        pltpu.make_async_copy(k_ref, o_all.at[1], local_sem.at[5]),
    ]
    for copy in local:
        copy.start()
    pl.semaphore_wait(barrier, len(friends))

    flow = Flow()

    def gather(kind, sends, megabytes, priority, source, target, ready):
        brought = {}
        for link, _, rel, chunk in sends:
            brought[(seen_by_receiver(link, rel), chunk)] = (kind, link, rel, chunk)
        first, after = {}, {}
        for link, _, rel, chunk in sends:
            name = flow.send(
                (kind, link, rel, chunk), link, priority(link, chunk), megabytes(chunk),
                lambda rel=rel, chunk=chunk: source(rel, chunk),
                lambda link=link, rel=rel, chunk=chunk: target(seen_by_receiver(link, rel), rel, chunk),
                lambda link=link: place.across(link),
            )
            if (rel, chunk) in brought:
                after.setdefault(brought[(rel, chunk)], []).append(name)
            else:
                assert not any(rel)
                first.setdefault(ready(chunk), []).append(name)
        for cause, names in first.items():
            flow.task((), 0.05, None, names, rank=0.5, after=cause)
        for cause, names in after.items():
            flow.task((cause,), 0.0, None, names, rank=0)
        return brought

    sends = []
    for matrix in range(2):
        sends += gather_tensor("W", matrix, ("x+", "x-")[matrix])

    def w_source(rel, matrix):
        return w_ref.at[matrix] if not any(rel) else w_all.at[matrix, place.tensor_at(rel)]

    w_from = gather(
        "W", sends, lambda matrix: out_slab * in_slab * 2e-6, lambda link, matrix: 1 + matrix,
        w_source, lambda _, rel, matrix: w_all.at[matrix, place.tensor_at(rel)], lambda matrix: (),
    )

    sends = []
    for chunk, (z_first, extra) in enumerate(X_MODES):
        sends += gather_dp("X", chunk, z_first, extra)

    def x_source(rel, chunk):
        rows = pl.ds(*cuts[chunk])
        return x_ref.at[rows, :] if not any(rel) else x_all.at[slot_of(rel), rows, :]

    x_from = gather(
        "X", sends, lambda chunk: cuts[chunk][1] * slab * 2e-6,
        lambda link, chunk: 10 + (link == "z" and not X_MODES[chunk][0]),
        x_source, lambda there, rel, chunk: x_all.at[slot_of(there), pl.ds(*cuts[chunk]), :], lambda chunk: (),
    )

    pair = 2 * out_slab

    def add_inner(rel, matrix, fresh, last):
        chip = place.tensor_at((rel[0], rel[1], 0)) // 2
        slabs = w_all[matrix, pl.ds(chip * 2, 2)].reshape(pair, in_slab)
        part = jnp.dot(o_all[matrix, :, aligned(chip * pair, pair)], slabs, preferred_element_type=jnp.float32)
        if not fresh:
            part = part + total[matrix]
        if last:
            inner_own[matrix] = part.astype(jnp.bfloat16)
        else:
            total[matrix] = part

    counts = {}

    def counted(key, times, run):
        def go():
            counts[key] = counts.get(key, 0) + 1
            run(counts[key] == 1, counts[key] == times)

        return go

    flow.task((), 0.3, lambda: [local[number].wait() for number in (1, 2, 3, 5)], rank=2, name=("w",))
    for matrix in range(2):
        units = []
        for rel in RELS:
            needs = [w_from[(rel + (core,), matrix)] for core in (0, 1) if any(rel) or core]
            units.append(("inner", rel, matrix))
            run = counted(
                ("inner", matrix), len(RELS),
                lambda fresh, last, rel=rel, matrix=matrix: add_inner(rel, matrix, fresh, last),
            )
            flow.task(needs, 0.6, run, rank=2 + matrix, after=(("w",),), name=units[-1])
        flow.task((), 0.0, None, rank=2, after=units, name=("inner", matrix))

    tiles = new_cols // TILE

    def e_columns(rel):
        return pl.ds(pl.multiple_of(place.dp_at(rel) * slab, 128), slab)

    def add_raw(rel, half, fresh):
        columns = e_columns(rel)

        def body(number, _):
            rows = aligned(number * TILE, TILE)
            block = x_all[slot_of(rel)] if any(rel) else x_pad[pl.ds(0, vocab_rows), :]
            part = lax.dot_general(block, e_all[rows, columns], LAST, preferred_element_type=jnp.float32)
            if fresh:
                raw[:, rows] = part
            else:
                raw[:, rows] += part
            return 0

        lax.fori_loop(half * tiles // 2, (half + 1) * tiles // 2, body, 0)

    raw_units = []
    for rel in RELS:
        for half in range(2):
            needs = [x_from[(rel, chunk)] for chunk in range(X_CUTS)] if any(rel) else []
            run = counted(
                ("raw", half), len(RELS), lambda fresh, last, rel=rel, half=half: add_raw(rel, half, fresh)
            )
            raw_units.append(("raw", rel, half))
            flow.task(needs, 1.3, run, rank=6, after=(("e",),), name=raw_units[-1])

    core_rows, chip_rows, own_rows = token_rows // 2, token_rows // 8, token_rows // 16
    mine = place.core * core_rows
    theirs = (1 - place.core) * core_rows

    def rows_of(core, shift, part=None):
        start = (1 - place.core if core else place.core) * core_rows + ((place.x + shift + 4) % 4) * chip_rows
        if part is None:
            return aligned(start, chip_rows)
        return aligned(start + part * own_rows, own_rows)

    def small_rows(flip):
        z_hi = 1 - place.z_hi if flip else place.z_hi
        return aligned(mine + place.x * chip_rows + z_hi * own_rows, own_rows)

    def lane_sums(values_ref, rows):
        sums = None
        for start in range(0, values_ref.shape[1], 128):
            part = jnp.square(values_ref[pl.ds(0, rows), start:start + 128].astype(jnp.float32))
            sums = part if sums is None else sums + part
        return sums

    def row_sums(values_ref):
        lanes[pl.ds(lanes.shape[0] - 32, 32), :] = jnp.zeros((32, 128), jnp.float32)
        lanes[pl.ds(0, vocab_rows), :] = lane_sums(values_ref, vocab_rows)
        return jnp.broadcast_to(jnp.sum(lanes[...].T, axis=0, keepdims=True), squares.shape)

    def load_x():
        local[0].wait()
        end = pl.ds(x_pad.shape[0] - 32, 32)
        row = lax.broadcasted_iota(jnp.int32, (32, slab), 0) + (x_pad.shape[0] - 32)
        x_pad[end, :] = jnp.where(row < vocab_rows, x_pad[end, :].astype(jnp.float32), 0.0).astype(jnp.bfloat16)

    def choose(start):
        def body(number, _):
            rows = aligned(start + number * TILE, TILE)
            ids = tokens_ref[rows, :] - place.tensor * vocab_rows
            column = lax.broadcasted_iota(jnp.int32, (TILE, x_pad.shape[0]), 1)
            one = jnp.where((ids == column) & (column < vocab_rows), 1.0, 0.0).astype(jnp.bfloat16)
            masked[rows, :] = jnp.dot(one, x_pad[...], preferred_element_type=jnp.float32).astype(jnp.bfloat16)
            return 0

        lax.fori_loop(0, core_rows // TILE, body, 0)

    def to(link):
        return lambda: place.across(link)

    core_mb = core_rows * slab * 2e-6
    block_mb = core_mb / 4
    flow.send("c1", "c", 0, core_mb, lambda: masked.at[aligned(theirs, core_rows), :], lambda: core_in, to("c"))
    flow.task((), 1.0, load_x, rank=1, name=("x",))
    flow.task((), 1.2, lambda: choose(theirs), ("c1",), rank=1, name=("theirs",), after=(("x",),))
    flow.task((), 1.2, lambda: choose(mine), rank=1, name=("mine",), after=(("theirs",),))

    def add_core():
        rows = aligned(mine, core_rows)
        masked[rows, :] += core_in[...]

    flow.send("r+", "x+", 0, block_mb / 2, lambda: masked.at[rows_of(0, 2, 0), :], lambda: left_in, to("x+"))
    flow.send("r-", "x-", 0, block_mb / 2, lambda: masked.at[rows_of(0, 2, 1), :], lambda: right_in, to("x-"))
    flow.task(("c1",), 0.5, add_core, ("r+", "r-"), rank=1, name=("core",), after=(("mine",),))

    def add_left():
        masked[rows_of(0, 1, 0), :] += left_in[...]

    def add_right():
        masked[rows_of(0, 3, 1), :] += right_in[...]

    flow.send("b+", "x+", 0, block_mb, lambda: masked.at[rows_of(0, 1), :], lambda: left_block, to("x+"))
    flow.send("b-", "x-", 0, block_mb, lambda: masked.at[rows_of(0, 3), :], lambda: right_block, to("x-"))
    flow.task(("r+",), 0.1, add_left, ("b+",), rank=1, after=(("core",),))
    flow.task(("r-",), 0.1, add_right, ("b-",), rank=1, after=(("core",),))

    def add_blocks():
        masked[rows_of(0, 0), :] += left_block[...] + right_block[...]

    flow.send("h1", "h", 0, block_mb / 2, lambda: masked.at[small_rows(1), :], lambda: half_in, to("h"))
    flow.task(("b+", "b-"), 0.2, add_blocks, ("h1",), rank=1, name=("blocks",), after=(("core",),))

    def add_half():
        chosen_all[0] = masked[small_rows(0), :] + half_in[...]

    flow.task(("h1",), 0.1, add_half, rank=1, name=("chosen",), after=(("blocks",),))
    t_from = gather(
        "T", gather_dp("T", 0, True, "y+"), lambda chunk: own_rows * slab * 2e-6, lambda link, chunk: 0,
        lambda rel, chunk: chosen_all.at[slot_of(rel) + 1], lambda there, rel, chunk: chosen_all.at[slot_of(there) + 1],
        lambda chunk: (("chosen",),),
    )

    def grow_chosen(rel, fresh, last):
        at = slot_of(rel) + 1
        columns = e_columns(rel)

        def body(number, _):
            rows = aligned(number * TILE, TILE)
            part = lax.dot_general(
                chosen_all[at], e_all[rows, columns], LAST, preferred_element_type=jnp.float32
            )
            if fresh:
                chosen_sum[:, rows] = part
            else:
                chosen_sum[:, rows] += part
            return 0

        lax.fori_loop(0, tiles, body, 0)
        if last:
            old_squares = None
            for number in range(N_DP):
                for start in range(0, slab, 128):
                    part = jnp.square(chosen_all[number, :, start:start + 128].astype(jnp.float32))
                    old_squares = part if old_squares is None else old_squares + part
            hidden[small_rows(0), pl.ds(0, new_cols)] = chosen_sum[...].astype(jnp.bfloat16)
            hidden[small_rows(0), pl.ds(new_cols, 128)] = old_squares.astype(jnp.bfloat16)

    units = []
    flow.task((), 0.1, lambda: local[4].wait(), rank=4, name=("e",))
    for rel in RELS:
        needs = [t_from[(rel, 0)]] if any(rel) else []
        run = counted("chosen", len(RELS), lambda fresh, last, rel=rel: grow_chosen(rel, fresh, last))
        units.append(("chosen", rel))
        flow.task(needs, 0.9, run, rank=1.5, after=(("e",), ("chosen",)), name=units[-1])

    own_mb = own_rows * hidden.shape[1] * 2e-6

    def same(name, link, megabytes, rows):
        return flow.send(
            name, link, 0, megabytes, lambda: hidden.at[rows(), :], lambda: hidden.at[rows(), :], to(link)
        )

    same("h2", "h", own_mb, lambda: small_rows(0))
    same("a+", "x+", 2 * own_mb, lambda: rows_of(0, 0))
    same("a-", "x-", 2 * own_mb, lambda: rows_of(0, 0))
    same("f+", "x+", own_mb, lambda: rows_of(0, 3, 0))
    same("f-", "x-", own_mb, lambda: rows_of(0, 1, 1))
    for shift in range(4):
        same(("c", shift), "c", 2 * own_mb, lambda shift=shift: rows_of(0, shift))
    flow.task((), 0.0, None, ("h2",), rank=0.5, after=units, name=("hidden",))
    flow.task(("h2",), 0.02, None, ("a+", "a-", ("c", 0)), rank=0.5, after=(("hidden",),))
    flow.task(("a+",), 0.0, None, ("f+", ("c", 3)), rank=0)
    flow.task(("a-",), 0.0, None, ("f-", ("c", 1)), rank=0)
    flow.task(("f+", "f-"), 0.0, None, (("c", 2),), rank=0)

    half = head_cols // 2
    sends = []
    for chunk, (z_first, extra) in enumerate(INNER_MODES):
        sends += gather_dp("I", chunk, z_first, extra)

    def inner_view(ref, chunk):
        return ref.at[chunk // 2, pl.ds((chunk % 2) * half, half), :]

    def i_source(rel, chunk):
        return inner_view(inner_all.at[slot_of(rel)] if any(rel) else inner_own, chunk)

    i_from = gather(
        "I", sends, lambda chunk: half * in_slab * 2e-6, lambda link, chunk: 3 + chunk // 2,
        i_source, lambda there, rel, chunk: inner_view(inner_all.at[slot_of(there)], chunk),
        lambda chunk: (("inner", chunk // 2),),
    )

    def add_grown(rel, matrix, fresh, last):
        columns = e_columns(rel)

        def body(number, _):
            rows = aligned(number * TILE, TILE)
            block = inner_all[slot_of(rel), matrix] if any(rel) else inner_own[matrix]
            part = lax.dot_general(e_all[rows, columns], block, LAST, preferred_element_type=jnp.float32)
            if not fresh:
                part = part + grown_sum[matrix, rows, :]
            if last:
                grown[matrix][rows, :] = part.astype(jnp.bfloat16)
            else:
                grown_sum[matrix, rows, :] = part
            return 0

        lax.fori_loop(0, tiles, body, 0)

    for matrix in range(2):
        units = []
        for rel in RELS:
            needs = [i_from[(rel, chunk)] for chunk in (2 * matrix, 2 * matrix + 1)] if any(rel) else []
            run = counted(
                ("grown", matrix), len(RELS),
                lambda fresh, last, rel=rel, matrix=matrix: add_grown(rel, matrix, fresh, last),
            )
            units.append(("grown", rel, matrix))
            flow.task(needs, 0.9, run, rank=3, after=(("e",), ("inner", matrix)), name=units[-1])
        flow.task((), 0.0, None, rank=3, after=units, name=("grown", matrix))

    def square_rows():
        row = lax.broadcasted_iota(jnp.int32, squares.shape, 0)
        squares[...] = jnp.where(row == 1, row_sums(x_pad), 0.0)
        squares[...] = jnp.where(row == 0, row_sums(raw), squares[...])

    square_sends = [
        flow.send(
            ("S", number), "far", 0, 0.03, lambda: squares, lambda number=number: squares_in.at[number],
            lambda rel=rel: (place.dp_at(rel), place.tensor),
        )
        for number, rel in enumerate(DP_PEERS)
    ]
    flow.task((), 2.5, square_rows, square_sends, rank=4, after=raw_units, name=("squares",))
    ge_cuts = ((0, slab, slot_of((1, 2))), (slab, new_cols - slab, slot_of((0, 2))))

    def ge_copies():
        return [
            pltpu.make_async_copy(
                x_all.at[slot, :, pl.ds(0, size)], ge_ref.at[:, pl.ds(start, size)], local_sem.at[6 + number]
            )
            for number, (start, size, slot) in enumerate(ge_cuts)
        ]

    def rescale():
        flow.wait_left([name for name in flow.sends if name[0] == "X"])
        sums = squares[...]
        for number in range(len(DP_PEERS)):
            sums = sums + squares_in[number]
        factor = jnp.sqrt((sums[1:2] / old_width + EMBED_EPSILON) / (sums[0:1] / new_width + EMBED_EPSILON))
        column = jnp.broadcast_to(factor, (128, factor.shape[1])).T[:vocab_rows]
        for start, size, slot in ge_cuts:
            for at in range(0, size, 128):
                scaled = raw[:, start + at:start + at + 128] * column
                x_all[slot, :, at:at + 128] = scaled.astype(jnp.bfloat16)
        for copy in ge_copies():
            copy.start()

    flow.task(square_sends, 2.5, rescale, rank=5, name=("scaled",), after=(("squares",),))

    def seq_rows(rel):
        return aligned(place.dp_at(rel) * per_seq, per_seq)

    def partial(rel, matrix):
        block = hidden[seq_rows(rel), pl.ds(0, new_cols)]
        return jnp.dot(block, grown[matrix][...], preferred_element_type=jnp.float32)

    def lane_squares_of(rel):
        sums = None
        for start in range(0, new_cols, 128):
            part = jnp.square(hidden[seq_rows(rel), start:start + 128].astype(jnp.float32))
            sums = part if sums is None else sums + part
        return sums

    def put_query(number, rel):
        q_out[number, :, :head_cols] = partial(rel, 0).astype(jnp.bfloat16)
        q_out[number, :, head_cols:] = lane_squares_of(rel).astype(jnp.bfloat16)

    def put_key(number, rel):
        k_out[number] = partial(rel, 1).astype(jnp.bfloat16)

    gathered = ["h2", "a+", "a-", "f+", "f-"] + [("c", shift) for shift in range(4)]
    arrivals = []
    for matrix, (put, out, into) in enumerate(((put_query, q_out, q_in), (put_key, k_out, k_in))):
        for number, rel in enumerate(DP_PEERS):
            name = flow.send(
                ("P", matrix, number), "far", 0, 0.1,
                lambda out=out, number=number: out.at[number], lambda into=into, number=number: into.at[number],
                lambda rel=rel: (place.dp_at(rel), place.tensor),
            )
            arrivals.append(name)
            flow.task(
                gathered, 0.4, lambda put=put, number=number, rel=rel: put(number, rel), (name,),
                rank=2.5, after=(("grown", matrix), ("hidden",)),
            )

    def keep_own(matrix):
        own_part[:, matrix * head_cols:(matrix + 1) * head_cols] = partial((0, 0), matrix)
        if matrix == 0:
            own_part[:, 2 * head_cols:] = lane_squares_of((0, 0))

    for matrix in range(2):
        flow.task(
            gathered, 0.4, lambda matrix=matrix: keep_own(matrix), rank=3.5,
            after=(("grown", matrix), ("hidden",)), name=("own", matrix),
        )

    def add_up():
        queries = own_part[:, :head_cols]
        keys = own_part[:, head_cols:2 * head_cols]
        square_lanes = own_part[:, 2 * head_cols:]
        for number in range(len(DP_PEERS)):
            queries = queries + q_in[number, :, :head_cols].astype(jnp.float32)
            square_lanes = square_lanes + q_in[number, :, head_cols:].astype(jnp.float32)
            keys = keys + k_in[number].astype(jnp.float32)
        raw_ms = jnp.sum(square_lanes, axis=1, keepdims=True) / new_width
        old_lanes = hidden[seq_rows((0, 0)), pl.ds(new_cols, 128)].astype(jnp.float32)
        old_ms = jnp.sum(old_lanes, axis=1, keepdims=True) / old_width
        factor = jnp.sqrt((old_ms + EMBED_EPSILON) / (raw_ms + EMBED_EPSILON))
        scale = factor * lax.rsqrt(factor * factor * raw_ms + TOKEN_EPSILON)
        both_ref[:, :head_cols] = queries * scale
        both_ref[:, head_cols:] = keys * scale

    flow.task(arrivals, 1.0, add_up, rank=9, after=(("own", 0), ("own", 1)))
    order = flow.arrange()
    flow.emit(order, send_sem, recv_sem)
    for copy in ge_copies():
        copy.wait()


def grow_and_check(token_ids, old_embed, expand_in, query_out, key_out, old_query, old_key):
    vocab_rows, slab = old_embed.shape
    in_slab, out_slab = old_query.shape
    new_cols = expand_in.shape[0]
    head_cols = query_out.shape[0]
    tokens = token_ids.shape[0]
    padded = -(-vocab_rows // 128) * 128
    per_seq = tokens // N_DP
    turned = jnp.stack([old_query.T, old_key.T])
    anywhere = pl.BlockSpec(memory_space=pl.ANY)
    inside = pl.BlockSpec(memory_space=pltpu.VMEM)
    bf16, f32 = jnp.bfloat16, jnp.float32
    count = (2 * 15) + 7 * X_CUTS + 7 * len(INNER_MODES) + 7 + 1 + 4 + 1 + 9 + 7 + 14
    return pl.pallas_call(
        lambda *refs: whole_kernel(D_NEW, *refs),
        out_shape=(
            jax.ShapeDtypeStruct((vocab_rows, new_cols), bf16),
            jax.ShapeDtypeStruct((new_cols, head_cols), bf16),
            jax.ShapeDtypeStruct((new_cols, head_cols), bf16),
            jax.ShapeDtypeStruct((per_seq, 2 * head_cols), f32),
        ),
        in_specs=[anywhere] * 5 + [inside],
        out_specs=(anywhere, inside, inside, inside),
        scratch_shapes=[
            pltpu.VMEM((padded, slab), bf16),
            pltpu.VMEM((N_DP - 1, vocab_rows, slab), bf16),
            pltpu.VMEM((vocab_rows, new_cols), f32),
            pltpu.VMEM((2, N_TENSOR, out_slab, in_slab), bf16),
            pltpu.VMEM(expand_in.shape, bf16),
            pltpu.VMEM((2,) + query_out.shape, bf16),
            pltpu.VMEM((2, head_cols, in_slab), f32),
            pltpu.VMEM((2, head_cols, in_slab), bf16),
            pltpu.VMEM((N_DP - 1, 2, head_cols, in_slab), bf16),
            pltpu.VMEM((2, new_cols, head_cols), f32),
            pltpu.VMEM((padded, 128), f32),
            pltpu.VMEM((8, padded), f32),
            pltpu.VMEM((7, 8, padded), f32),
            pltpu.VMEM((tokens, slab), bf16),
            pltpu.VMEM((tokens // 2, slab), bf16),
            pltpu.VMEM((tokens // 16, slab), bf16),
            pltpu.VMEM((tokens // 16, slab), bf16),
            pltpu.VMEM((tokens // 8, slab), bf16),
            pltpu.VMEM((tokens // 8, slab), bf16),
            pltpu.VMEM((tokens // 16, slab), bf16),
            pltpu.VMEM((N_DP, tokens // 16, slab), bf16),
            pltpu.VMEM((tokens // 16, new_cols), f32),
            pltpu.VMEM((tokens, new_cols + 128), bf16),
            pltpu.VMEM((7, per_seq, head_cols + 128), bf16),
            pltpu.VMEM((7, per_seq, head_cols + 128), bf16),
            pltpu.VMEM((7, per_seq, head_cols), bf16),
            pltpu.VMEM((7, per_seq, head_cols), bf16),
            pltpu.VMEM((per_seq, 2 * head_cols + 128), f32),
            pltpu.SemaphoreType.DMA((count,)),
            pltpu.SemaphoreType.DMA((count,)),
            pltpu.SemaphoreType.DMA((8,)),
        ],
        compiler_params=pltpu.CompilerParams(
            collective_id=1, has_side_effects=True, vmem_limit_bytes=VMEM_LIMIT
        ),
        name="grow_and_check",
    )(old_embed, turned, expand_in, query_out, key_out, token_ids.reshape(tokens, 1))


def rotate(values, head_count):
    row_count = values.shape[0]
    shaped = values.reshape(row_count, head_count, HEAD)
    half_size = HEAD // 2
    position = jnp.arange(row_count).astype(jnp.float32)
    frequency = jnp.exp(
        -math.log(10000.0) * jnp.arange(half_size).astype(jnp.float32) * (2.0 / HEAD)
    )
    angles = position[:, None] * frequency[None, :]
    cosine = jnp.cos(angles)[:, None, :]
    sine_table = jnp.sin(angles)[:, None, :]
    first_half = shaped[..., :half_size]
    second = shaped[..., half_size:]
    return jnp.concatenate(
        [first_half * cosine - second * sine_table, second * cosine + first_half * sine_table],
        axis=-1,
    )


def entropy_of(queries, key_proj, head_count):
    rotated_q = rotate(queries, head_count).astype(jnp.bfloat16)
    rotated_k = rotate(key_proj, head_count).astype(jnp.bfloat16)
    scores = jnp.einsum(
        "ihd,jhd->hij", rotated_q, rotated_k, preferred_element_type=jnp.float32
    ) * HEAD ** (-0.5)
    row_count = queries.shape[0]
    causal = jnp.arange(row_count)[:, None] >= jnp.arange(row_count)[None, :]
    weights = jnp.where(causal[None], jnp.exp(scores), 0.0)
    weight_sum = jnp.sum(weights, axis=-1)
    entropy = jnp.log(weight_sum) - jnp.sum(weights * scores, axis=-1) / weight_sum
    return entropy.T


def on_device(token_ids, old_embed, expand_in, query_out, key_out, old_query, old_key):
    head_cols = query_out.shape[0]
    grown_embedding, grown_query, grown_key, both = grow_and_check(
        token_ids, old_embed, expand_in, query_out, key_out, old_query, old_key
    )
    attention_entropy = entropy_of(both[:, :head_cols], both[:, head_cols:], head_cols // HEAD)
    return (grown_embedding, grown_query, grown_key, attention_entropy)


def solution(mesh):
    placed = (
        P(),
        P("tensor", "dp"),
        P("dp", None),
        P("tensor", None),
        P("tensor", None),
        P("dp", "tensor"),
        P("dp", "tensor"),
    )
    return jax.shard_map(
        on_device,
        mesh=mesh,
        in_specs=placed,
        out_specs=(P("tensor", "dp"), P("dp", "tensor"), P("dp", "tensor"), P("dp", "tensor")),
        check_vma=False,
    )
```

time: 623 us -> 173 us (0.28)
  waiting for transfers between devices: 509 us -> 0 us
  Pallas kernels: 0 us -> 161 us
  matrix products: 55.7 us -> 0.27 us
  blocking collectives: 17.2 us -> 0 us
  between operations: 14.3 us -> 0.72 us
  other arithmetic: 10.8 us -> 3.08 us
    all_gather x7 -> x0, waiting for transfers between devices: 333 us -> none  [the longest x1 103 us: on_device(): shard_piece = lax.all_gather(old_embed, 'dp', axis=1, tiled=True)]
    pallas_call x0 -> x1, Pallas kernels: none -> 161 us  [grow_and_check(): pl.pallas_call(lambda *refs: whole_kernel(D_NEW, *refs), out_shape=(jax.S...]
    psum x1 -> x0, waiting for transfers between devices: 139 us -> none  [on_device(): hidden_cols = lax.psum(partial_rows.astype(jnp.bfloat16), 'tensor')]
    dot_general x7 -> x0, matrix products: 55.4 us -> none  [the longest x5 47.4 us: contract_last(): lax.dot_general(left_side, right_side, (((1,), (1,)), ((), ())), preferre...]
    all_to_all x1 -> x0, waiting for transfers between devices: 35.1 us -> none  [on_device(): lax.all_to_all(hidden_cols, 'dp', split_axis=0, concat_axis=1, tiled=True)]
    psum x1 -> x0, blocking collectives: 17.2 us -> none  [on_device(): new_squares = lax.psum(jnp.sum(jnp.square(raw_rows), axis=1), 'dp')]
    reduce_sum x2 -> x0, other arithmetic: 7.3 us -> none  [the longest x1 6.21 us: on_device(): old_squares = jnp.sum(jnp.square(shard_piece.astype(jnp.float32)), axis=1)]
  transfers between devices with their start and end apart: 9 -> 0, of which waited for: 8 -> 0; matrix products, arithmetic and copies ran while one was open for 11% -> 0% of each run, Pallas kernels for 0% -> 0%
where the time goes in v3:
time: 173 us; the launch traced here: 171 us
  Pallas kernels  161 us (93%)
  local copies, waits for them, and re-layouts  6.21 us (4%)
  other arithmetic  3.08 us (2%)
    pallas_call x1, Pallas kernels, grow_and_check(): pl.pallas_call(lambda *refs: whole_kernel(D_NEW, *refs), out_shape=(jax.S...  161 us

profile of v3, /device:TPU:0, one launch (start us, length us, event | category | flops | bytes accessed | tf_op | source)
XLA Modules:
  0.0 170.8 jit_solution(9439205013787434117)
XLA Ops:
  0.6 2.1 %pad_maximum_fusion.refs_1_ = bf16[2,320,640]{2,1,0:T(8,128)(2,1)} fusion(bf16[1,320,640]{2,1,0:T(8,128)(2,1)} %bitcast.9, bf16[1,320,640]{2,1,0:T(8,128)(2,1)} %bitcast.10), kind=kLoop, calls=%fused_computation.1 | loop fusion | flops 409600 | bytes 1638400 | tf_op jit(solution)/shard_map/stack | solution.py:687
  2.7 1.7 copy.15.refs_5_
  4.4 160.5 %grow_and_check.1 = (bf16[1000,1024]{1,0:T(8,128)(2,1)}, bf16[1024,256]{1,0:T(8,128)(2,1)}, bf16[1024,256]{1,0:T(8,128)(2,1)}, f32[128,512]{1,0:T(8,128)}) custom-call(bf16[1000,640]{1,0:T(8,128)(2,1)} %refs_0_.1, bf16[2,320,640]{2,1,0:T(8,128)(2,1)} %pad_maximum_fusion.refs_1_, bf16[1024,5120]{1,0:T(8,128)(2,1)} %refs_2_.1, bf16[256,5120]{1,0:T(8,128)(2,1)} %refs_3_.1, ...), custom_call_target="tpu_custom_call" | custom-call | tf_op jit(solution)/shard_map/grow_and_check/pallas_call | solution.py:692
  164.9 0.0 copy-start
  165.0 1.1 fusion.8
  166.1 0.1 reshape.87
  166.2 0.1 reshape.88
  166.3 0.3 fusion.9
  166.6 0.3 multiply_cosine_fusion
  166.9 0.0 copy-start.2
  166.9 0.1 subtract_convert_fusion
  167.0 0.3 fusion
  167.3 0.0 copy-start.1
  167.3 0.6 subtract_bitcast_fusion
  167.9 0.0 copy-done
  167.9 1.3 copy.35
  169.2 0.0 copy-done.2
  169.2 0.8 copy.36
  170.0 0.0 copy-done.1
  170.0 0.8 copy.37
  (3 shorter events, 0.0 us)
Async XLA Ops:
  164.9 2.9 %copy-start = (bf16[1000,1024]{1,0:T(8,128)(2,1)S(1)}, bf16[1000,1024]{1,0:T(8,128)(2,1)}, u32[]{:S(2)}) copy-start(bf16[1000,1024]{1,0:T(8,128)(2,1)} %get-tuple-element.34) | copy-start | bytes 6144004
  166.9 2.3 %copy-start.2 = (bf16[1024,256]{1,0:T(8,128)(2,1)S(1)}, bf16[1024,256]{1,0:T(8,128)(2,1)}, u32[]{:S(2)}) copy-start(bf16[1024,256]{1,0:T(8,128)(2,1)} %get-tuple-element.35) | copy-start | bytes 1572868
  167.3 2.7 %copy-start.1 = (bf16[1024,256]{1,0:T(8,128)(2,1)S(1)}, bf16[1024,256]{1,0:T(8,128)(2,1)}, u32[]{:S(2)}) copy-start(bf16[1024,256]{1,0:T(8,128)(2,1)} %get-tuple-element.36) | copy-start | bytes 1572868

commit v4 on v3

--- a/solution.py
+++ b/solution.py
@@ -104,9 +104,9 @@
         self.tasks = []
         self.left_already = set()
 
-    def send(self, name, link, priority, megabytes, source, target, to):
+    def send(self, name, link, priority, megabytes, source, target, to, over=()):
         assert name not in self.sends
-        self.sends[name] = (link, priority, megabytes, source, target, to)
+        self.sends[name] = (link, priority, megabytes, source, target, to, over)
         return name
 
     def task(self, needs, cost, run, sends=(), rank=5, after=(), name=None):
@@ -122,8 +122,11 @@
             while queues.get(link) and flying.get(link, 0) < DEPTH.get(link, 1000):
                 name = heapq.heappop(queues[link])[2]
                 flying[link] = flying.get(link, 0) + 1
-                free[link] = max(free.get(link, 0.0), now) + self.sends[name][2] / LINK_RATES[link]
-                heapq.heappush(heap, (free[link] + 1.5, len(order), name))
+                over = self.sends[name][6] + (("z",) if link == "h" else ())
+                for each in (link,) + over:
+                    free[each] = max(free.get(each, 0.0), now) + self.sends[name][2] / LINK_RATES[each]
+                there = max(free[each] for each in (link,) + over)
+                heapq.heappush(heap, (there + LATENCY.get(link, HOP), len(order), name))
                 order.append(("start", name))
 
         while left or heap:
@@ -172,7 +175,7 @@
         return order
 
     def copy_of(self, name):
-        _, _, _, source, target, to = self.sends[name]
+        _, _, _, source, target, to, _ = self.sends[name]
         number = self.number_of[name]
         return pltpu.make_async_remote_copy(
             src_ref=source(),
@@ -206,11 +209,18 @@
         self.wait_left(list(self.sends))
 
 
-DEPTH = {"y+": 3, "y-": 3, "z": 3, "x+": 3, "x-": 3, "h": 3}
+DEPTH = {"y+": 3, "y-": 3, "z": 3, "x+": 2, "x-": 2, "h": 2}
 LINK_RATES = {
-    "y+": 0.0465, "y-": 0.0465, "z": 0.0465, "x+": 0.0465, "x-": 0.0465, "h": 0.0465, "c": 0.3, "far": 0.03,
+    "y+": 0.0455, "y-": 0.0455, "z": 0.0455, "x+": 0.0455, "x-": 0.0455, "h": 0.0455, "c": 0.12, "far": 0.5, "s": 0.2,
+}
+HOP = 2.5
+LATENCY = {"h": 3.5}
+PEER_OVER = {
+    (1, 2): ("z", "y+"), (0, 2): ("y+", "y-"), (1, 1): ("z", "y+"), (1, 3): ("z", "y-"),
+    (1, 0): ("z",), (0, 1): ("y+",), (0, 3): ("y-",),
 }
 DP_PEERS = ((1, 2), (0, 2), (1, 1), (1, 3), (1, 0), (0, 1), (0, 3))
+W_PARTS = 2
 X_CUTS = 7
 X_MODES = ((False, "y+"), (False, "y-"), (True, "y+"), (True, "y-"), (True, "y+"), (True, "y-"), (True, "y+"))
 INNER_MODES = ((True, "y+"), (False, "y-"), (True, "y-"), (False, "y+"))
@@ -240,7 +250,7 @@
     new_cols, old_width = e_ref.shape
     new_width = sizes
     head_cols = q_ref.shape[0]
-    token_rows = tokens_ref.shape[0]
+    token_rows = tokens_ref.shape[1]
     out_slab, in_slab = w_ref.shape[1:]
     grown = (gq_ref, gk_ref)
     per_seq = both_ref.shape[0]
@@ -290,15 +300,20 @@
         return brought
 
     sends = []
-    for matrix in range(2):
-        sends += gather_tensor("W", matrix, ("x+", "x-")[matrix])
-
-    def w_source(rel, matrix):
-        return w_ref.at[matrix] if not any(rel) else w_all.at[matrix, place.tensor_at(rel)]
+    for chunk in range(2 * W_PARTS):
+        sends += gather_tensor("W", chunk, ("x+", "x-")[chunk % 2])
+    w_rows = out_slab // W_PARTS
+
+    def w_view(ref, chunk):
+        return ref.at[pl.ds((chunk % W_PARTS) * w_rows, w_rows), :]
+
+    def w_target(rel, chunk):
+        return w_view(w_all.at[chunk // W_PARTS, place.tensor_at(rel)], chunk)
 
     w_from = gather(
-        "W", sends, lambda matrix: out_slab * in_slab * 2e-6, lambda link, matrix: 1 + matrix,
-        w_source, lambda _, rel, matrix: w_all.at[matrix, place.tensor_at(rel)], lambda matrix: (),
+        "W", sends, lambda chunk: w_rows * in_slab * 2e-6, lambda link, chunk: 1 + chunk // W_PARTS,
+        lambda rel, chunk: w_target(rel, chunk) if any(rel) else w_view(w_ref.at[chunk // W_PARTS], chunk),
+        lambda _, rel, chunk: w_target(rel, chunk), lambda chunk: (),
     )
 
     sends = []
@@ -341,7 +356,10 @@
     for matrix in range(2):
         units = []
         for rel in RELS:
-            needs = [w_from[(rel + (core,), matrix)] for core in (0, 1) if any(rel) or core]
+            needs = [
+                w_from[(rel + (core,), matrix * W_PARTS + part)]
+                for core in (0, 1) for part in range(W_PARTS) if any(rel) or core
+            ]
             units.append(("inner", rel, matrix))
             run = counted(
                 ("inner", matrix), len(RELS),
@@ -415,7 +433,8 @@
     def choose(start):
         def body(number, _):
             rows = aligned(start + number * TILE, TILE)
-            ids = tokens_ref[rows, :] - place.tensor * vocab_rows
+            row = jnp.broadcast_to(tokens_ref[:, rows].astype(jnp.float32), (128, TILE))
+            ids = row.T[:, :1].astype(jnp.int32) - place.tensor * vocab_rows
             column = lax.broadcasted_iota(jnp.int32, (TILE, x_pad.shape[0]), 1)
             one = jnp.where((ids == column) & (column < vocab_rows), 1.0, 0.0).astype(jnp.bfloat16)
             masked[rows, :] = jnp.dot(one, x_pad[...], preferred_element_type=jnp.float32).astype(jnp.bfloat16)
@@ -574,7 +593,7 @@
 
     square_sends = [
         flow.send(
-            ("S", number), "far", 0, 0.03, lambda: squares, lambda number=number: squares_in.at[number],
+            ("S", number), "s", 0, 0.03, lambda: squares, lambda number=number: squares_in.at[number],
             lambda rel=rel: (place.dp_at(rel), place.tensor),
         )
         for number, rel in enumerate(DP_PEERS)
@@ -632,9 +651,9 @@
     for matrix, (put, out, into) in enumerate(((put_query, q_out, q_in), (put_key, k_out, k_in))):
         for number, rel in enumerate(DP_PEERS):
             name = flow.send(
-                ("P", matrix, number), "far", 0, 0.1,
+                ("P", matrix, number), "far", 0, per_seq * out.shape[2] * 2e-6,
                 lambda out=out, number=number: out.at[number], lambda into=into, number=number: into.at[number],
-                lambda rel=rel: (place.dp_at(rel), place.tensor),
+                lambda rel=rel: (place.dp_at(rel), place.tensor), PEER_OVER[rel],
             )
             arrivals.append(name)
             flow.task(
@@ -688,7 +707,7 @@
     anywhere = pl.BlockSpec(memory_space=pl.ANY)
     inside = pl.BlockSpec(memory_space=pltpu.VMEM)
     bf16, f32 = jnp.bfloat16, jnp.float32
-    count = (2 * 15) + 7 * X_CUTS + 7 * len(INNER_MODES) + 7 + 1 + 4 + 1 + 9 + 7 + 14
+    count = (2 * W_PARTS * 15) + 7 * X_CUTS + 7 * len(INNER_MODES) + 7 + 1 + 4 + 1 + 9 + 7 + 14
     return pl.pallas_call(
         lambda *refs: whole_kernel(D_NEW, *refs),
         out_shape=(
@@ -736,7 +755,7 @@
             collective_id=1, has_side_effects=True, vmem_limit_bytes=VMEM_LIMIT
         ),
         name="grow_and_check",
-    )(old_embed, turned, expand_in, query_out, key_out, token_ids.reshape(tokens, 1))
+    )(old_embed, turned, expand_in, query_out, key_out, token_ids.reshape(1, tokens))
 
 
 def rotate(values, head_count):

time: 173 us -> 153 us (0.88)
  Pallas kernels: 161 us -> 143 us
    pallas_call x1, Pallas kernels: 161 us -> 143 us  [grow_and_check(): pl.pallas_call(lambda *refs: whole_kernel(D_NEW, *refs), out_shape=(jax.S...]
where the time goes in v4:
time: 153 us; the launch traced here: 152 us
  Pallas kernels  143 us (93%)
  local copies, waits for them, and re-layouts  4.51 us (3%)
  other arithmetic  3.08 us (2%)
    pallas_call x1, Pallas kernels, grow_and_check(): pl.pallas_call(lambda *refs: whole_kernel(D_NEW, *refs), out_shape=(jax.S...  143 us

profile of v4, /device:TPU:0, one launch (start us, length us, event | category | flops | bytes accessed | tf_op | source)
XLA Modules:
  0.0 151.8 jit_solution(7783544717511267329)
XLA Ops:
  0.6 2.1 %pad_maximum_fusion.refs_1_ = bf16[2,320,640]{2,1,0:T(8,128)(2,1)} fusion(bf16[1,320,640]{2,1,0:T(8,128)(2,1)} %bitcast.9, bf16[1,320,640]{2,1,0:T(8,128)(2,1)} %bitcast.10), kind=kLoop, calls=%fused_computation.1 | loop fusion | flops 409600 | bytes 1638400 | tf_op jit(solution)/shard_map/stack | solution.py:706
  2.7 143.2 %grow_and_check.1 = (bf16[1000,1024]{1,0:T(8,128)(2,1)}, bf16[1024,256]{1,0:T(8,128)(2,1)}, bf16[1024,256]{1,0:T(8,128)(2,1)}, f32[128,512]{1,0:T(8,128)}) custom-call(bf16[1000,640]{1,0:T(8,128)(2,1)} %refs_0_.1, bf16[2,320,640]{2,1,0:T(8,128)(2,1)} %pad_maximum_fusion.refs_1_, bf16[1024,5120]{1,0:T(8,128)(2,1)} %refs_2_.1, bf16[256,5120]{1,0:T(8,128)(2,1)} %refs_3_.1, ...), custom_call_target="tpu_custom_call" | custom-call | tf_op jit(solution)/shard_map/grow_and_check/pallas_call | solution.py:711
  145.9 0.0 copy-start
  145.9 1.1 fusion.8
  147.1 0.1 reshape.87
  147.1 0.1 reshape.88
  147.2 0.3 fusion.9
  147.6 0.3 multiply_cosine_fusion
  147.9 0.0 copy-start.2
  147.9 0.1 subtract_convert_fusion
  148.0 0.3 fusion
  148.3 0.0 copy-start.1
  148.3 0.6 subtract_bitcast_fusion
  148.9 0.0 copy-done
  148.9 1.3 copy.30
  150.2 0.0 copy-done.2
  150.2 0.8 copy.31
  151.0 0.0 copy-done.1
  151.0 0.8 copy.32
  (3 shorter events, 0.0 us)
Async XLA Ops:
  145.9 3.0 %copy-start = (bf16[1000,1024]{1,0:T(8,128)(2,1)S(1)}, bf16[1000,1024]{1,0:T(8,128)(2,1)}, u32[]{:S(2)}) copy-start(bf16[1000,1024]{1,0:T(8,128)(2,1)} %get-tuple-element.34) | copy-start | bytes 6144004
  147.9 2.3 %copy-start.2 = (bf16[1024,256]{1,0:T(8,128)(2,1)S(1)}, bf16[1024,256]{1,0:T(8,128)(2,1)}, u32[]{:S(2)}) copy-start(bf16[1024,256]{1,0:T(8,128)(2,1)} %get-tuple-element.35) | copy-start | bytes 1572868
  148.3 2.7 %copy-start.1 = (bf16[1024,256]{1,0:T(8,128)(2,1)S(1)}, bf16[1024,256]{1,0:T(8,128)(2,1)}, u32[]{:S(2)}) copy-start(bf16[1024,256]{1,0:T(8,128)(2,1)} %get-tuple-element.36) | copy-start | bytes 1572868

commit v5 on v4

--- a/solution.py
+++ b/solution.py
@@ -196,15 +196,23 @@
         self.number_of = {name: number for number, name in enumerate(self.sends)}
         self.send_sem, self.recv_sem = send_sem, recv_sem
         arrived, started = set(), set()
+        needed = {send: needs for needs, _, _, sends, _, _, _ in self.tasks for send in sends}
+
+        def wait_for(names):
+            for name in sorted(names - arrived, key=str):
+                self.copy_of(name).wait_recv()
+                arrived.add(name)
+
         for what, which in order:
-            if what == "arrive":
-                self.copy_of(which).wait_recv()
-                arrived.add(which)
-            elif what == "start":
+            if what == "start":
+                wait_for(needed[which])
                 self.copy_of(which).start()
                 started.add(which)
-            elif self.tasks[which][2] is not None:
-                self.tasks[which][2]()
+            elif what == "run":
+                wait_for(self.tasks[which][0])
+                if self.tasks[which][2] is not None:
+                    self.tasks[which][2]()
+        wait_for(set(self.sends))
         assert arrived == set(self.sends) and started == set(self.sends)
         self.wait_left(list(self.sends))
 
@@ -242,7 +250,7 @@
     x_pad, x_all, raw, w_all, e_all, o_all, total, inner_own, inner_all, grown_sum,
     lanes, squares, squares_in,
     masked, core_in, left_in, right_in, left_block, right_block, half_in, chosen_all, chosen_sum, hidden,
-    q_out, q_in, k_out, k_in, own_part,
+    q_out, q_in, k_out, k_in, own_part, chunk_squares, chunk_in,
     send_sem, recv_sem, local_sem,
 ):
     place = Place()
@@ -504,13 +512,37 @@
 
         lax.fori_loop(0, tiles, body, 0)
         if last:
-            old_squares = None
-            for number in range(N_DP):
-                for start in range(0, slab, 128):
-                    part = jnp.square(chosen_all[number, :, start:start + 128].astype(jnp.float32))
-                    old_squares = part if old_squares is None else old_squares + part
-            hidden[small_rows(0), pl.ds(0, new_cols)] = chosen_sum[...].astype(jnp.bfloat16)
-            hidden[small_rows(0), pl.ds(new_cols, 128)] = old_squares.astype(jnp.bfloat16)
+            sums = None
+            for start in range(0, new_cols, 128):
+                part = jnp.square(chosen_sum[:, start:start + 128])
+                sums = part if sums is None else sums + part
+            lanes[pl.ds(0, own_rows), :] = sums
+            lanes[pl.ds(own_rows, 128 - own_rows), :] = jnp.zeros((128 - own_rows, 128), jnp.float32)
+            row = jnp.sum(lanes[pl.ds(0, 128), :].T, axis=0, keepdims=True)
+            chunk_squares[...] = jnp.broadcast_to(row, chunk_squares.shape)
+
+    def scale_chosen():
+        row = chunk_squares[...]
+        for number in range(len(DP_PEERS)):
+            row = row + chunk_in[number]
+        raw_ms = jnp.broadcast_to(row[:1], (128, 128)).T[:own_rows, :1] / new_width
+        old_squares = None
+        for number in range(N_DP):
+            for start in range(0, slab, 128):
+                part = jnp.square(chosen_all[number, :, start:start + 128].astype(jnp.float32))
+                old_squares = part if old_squares is None else old_squares + part
+        old_ms = jnp.sum(old_squares, axis=1, keepdims=True) / old_width
+        factor = jnp.sqrt((old_ms + EMBED_EPSILON) / (raw_ms + EMBED_EPSILON))
+        scale = factor * lax.rsqrt(factor * factor * raw_ms + TOKEN_EPSILON)
+        hidden[small_rows(0), :] = (chosen_sum[...] * scale).astype(jnp.bfloat16)
+
+    chunk_sends = [
+        flow.send(
+            ("Q", number), "s", 0, 0.004, lambda: chunk_squares, lambda number=number: chunk_in.at[number],
+            lambda rel=rel: (place.dp_at(rel), place.tensor),
+        )
+        for number, rel in enumerate(DP_PEERS)
+    ]
 
     units = []
     flow.task((), 0.1, lambda: local[4].wait(), rank=4, name=("e",))
@@ -534,7 +566,8 @@
     same("f-", "x-", own_mb, lambda: rows_of(0, 1, 1))
     for shift in range(4):
         same(("c", shift), "c", 2 * own_mb, lambda shift=shift: rows_of(0, shift))
-    flow.task((), 0.0, None, ("h2",), rank=0.5, after=units, name=("hidden",))
+    flow.task((), 0.0, None, chunk_sends, rank=0.5, after=units, name=("chunk",))
+    flow.task(chunk_sends, 0.5, scale_chosen, ("h2",), rank=0.5, after=(("chunk",),), name=("hidden",))
     flow.task(("h2",), 0.02, None, ("a+", "a-", ("c", 0)), rank=0.5, after=(("hidden",),))
     flow.task(("a+",), 0.0, None, ("f+", ("c", 3)), rank=0)
     flow.task(("a-",), 0.0, None, ("f-", ("c", 1)), rank=0)
@@ -629,19 +662,11 @@
         return aligned(place.dp_at(rel) * per_seq, per_seq)
 
     def partial(rel, matrix):
-        block = hidden[seq_rows(rel), pl.ds(0, new_cols)]
+        block = hidden[seq_rows(rel), :]
         return jnp.dot(block, grown[matrix][...], preferred_element_type=jnp.float32)
 
-    def lane_squares_of(rel):
-        sums = None
-        for start in range(0, new_cols, 128):
-            part = jnp.square(hidden[seq_rows(rel), start:start + 128].astype(jnp.float32))
-            sums = part if sums is None else sums + part
-        return sums
-
     def put_query(number, rel):
-        q_out[number, :, :head_cols] = partial(rel, 0).astype(jnp.bfloat16)
-        q_out[number, :, head_cols:] = lane_squares_of(rel).astype(jnp.bfloat16)
+        q_out[number] = partial(rel, 0).astype(jnp.bfloat16)
 
     def put_key(number, rel):
         k_out[number] = partial(rel, 1).astype(jnp.bfloat16)
@@ -663,8 +688,6 @@
 
     def keep_own(matrix):
         own_part[:, matrix * head_cols:(matrix + 1) * head_cols] = partial((0, 0), matrix)
-        if matrix == 0:
-            own_part[:, 2 * head_cols:] = lane_squares_of((0, 0))
 
     for matrix in range(2):
         flow.task(
@@ -673,20 +696,12 @@
         )
 
     def add_up():
-        queries = own_part[:, :head_cols]
-        keys = own_part[:, head_cols:2 * head_cols]
-        square_lanes = own_part[:, 2 * head_cols:]
-        for number in range(len(DP_PEERS)):
-            queries = queries + q_in[number, :, :head_cols].astype(jnp.float32)
-            square_lanes = square_lanes + q_in[number, :, head_cols:].astype(jnp.float32)
-            keys = keys + k_in[number].astype(jnp.float32)
-        raw_ms = jnp.sum(square_lanes, axis=1, keepdims=True) / new_width
-        old_lanes = hidden[seq_rows((0, 0)), pl.ds(new_cols, 128)].astype(jnp.float32)
-        old_ms = jnp.sum(old_lanes, axis=1, keepdims=True) / old_width
-        factor = jnp.sqrt((old_ms + EMBED_EPSILON) / (raw_ms + EMBED_EPSILON))
-        scale = factor * lax.rsqrt(factor * factor * raw_ms + TOKEN_EPSILON)
-        both_ref[:, :head_cols] = queries * scale
-        both_ref[:, head_cols:] = keys * scale
+        for matrix, into in enumerate((q_in, k_in)):
+            columns = pl.ds(matrix * head_cols, head_cols)
+            sums = own_part[:, columns]
+            for number in range(len(DP_PEERS)):
+                sums = sums + into[number].astype(jnp.float32)
+            both_ref[:, columns] = sums
 
     flow.task(arrivals, 1.0, add_up, rank=9, after=(("own", 0), ("own", 1)))
     order = flow.arrange()
@@ -707,7 +722,7 @@
     anywhere = pl.BlockSpec(memory_space=pl.ANY)
     inside = pl.BlockSpec(memory_space=pltpu.VMEM)
     bf16, f32 = jnp.bfloat16, jnp.float32
-    count = (2 * W_PARTS * 15) + 7 * X_CUTS + 7 * len(INNER_MODES) + 7 + 1 + 4 + 1 + 9 + 7 + 14
+    count = (2 * W_PARTS * 15) + 7 * X_CUTS + 7 * len(INNER_MODES) + 7 + 1 + 4 + 1 + 9 + 7 + 14 + 7
     return pl.pallas_call(
         lambda *refs: whole_kernel(D_NEW, *refs),
         out_shape=(
@@ -741,12 +756,14 @@
             pltpu.VMEM((tokens // 16, slab), bf16),
             pltpu.VMEM((N_DP, tokens // 16, slab), bf16),
             pltpu.VMEM((tokens // 16, new_cols), f32),
-            pltpu.VMEM((tokens, new_cols + 128), bf16),
-            pltpu.VMEM((7, per_seq, head_cols + 128), bf16),
-            pltpu.VMEM((7, per_seq, head_cols + 128), bf16),
+            pltpu.VMEM((tokens, new_cols), bf16),
             pltpu.VMEM((7, per_seq, head_cols), bf16),
             pltpu.VMEM((7, per_seq, head_cols), bf16),
-            pltpu.VMEM((per_seq, 2 * head_cols + 128), f32),
+            pltpu.VMEM((7, per_seq, head_cols), bf16),
+            pltpu.VMEM((7, per_seq, head_cols), bf16),
+            pltpu.VMEM((per_seq, 2 * head_cols), f32),
+            pltpu.VMEM((8, 128), f32),
+            pltpu.VMEM((7, 8, 128), f32),
             pltpu.SemaphoreType.DMA((count,)),
             pltpu.SemaphoreType.DMA((count,)),
             pltpu.SemaphoreType.DMA((8,)),

time: 153 us -> 148 us (0.967)
  Pallas kernels: 143 us -> 139 us
    pallas_call x1, Pallas kernels: 143 us -> 139 us  [grow_and_check(): pl.pallas_call(lambda *refs: whole_kernel(D_NEW, *refs), out_shape=(jax.S...]
where the time goes in v5:
time: 148 us
  Pallas kernels  139 us (94%)
  local copies, waits for them, and re-layouts  4.51 us (3%)
  other arithmetic  3.08 us (2%)
    pallas_call x1, Pallas kernels, grow_and_check(): pl.pallas_call(lambda *refs: whole_kernel(D_NEW, *refs), out_shape=(jax.S...  139 us

profile of v5, /device:TPU:0, one launch (start us, length us, event | category | flops | bytes accessed | tf_op | source)
XLA Modules:
  0.0 147.7 jit_solution(9207005398991698432)
XLA Ops:
  0.6 2.1 %pad_maximum_fusion.refs_1_ = bf16[2,320,640]{2,1,0:T(8,128)(2,1)} fusion(bf16[1,320,640]{2,1,0:T(8,128)(2,1)} %bitcast.9, bf16[1,320,640]{2,1,0:T(8,128)(2,1)} %bitcast.10), kind=kLoop, calls=%fused_computation.1 | loop fusion | flops 409600 | bytes 1638400 | tf_op jit(solution)/shard_map/stack | solution.py:721
  2.7 139.1 %grow_and_check.1 = (bf16[1000,1024]{1,0:T(8,128)(2,1)}, bf16[1024,256]{1,0:T(8,128)(2,1)}, bf16[1024,256]{1,0:T(8,128)(2,1)}, f32[128,512]{1,0:T(8,128)}) custom-call(bf16[1000,640]{1,0:T(8,128)(2,1)} %refs_0_.1, bf16[2,320,640]{2,1,0:T(8,128)(2,1)} %pad_maximum_fusion.refs_1_, bf16[1024,5120]{1,0:T(8,128)(2,1)} %refs_2_.1, bf16[256,5120]{1,0:T(8,128)(2,1)} %refs_3_.1, ...), custom_call_target="tpu_custom_call" | custom-call | tf_op jit(solution)/shard_map/grow_and_check/pallas_call | solution.py:726
  141.9 0.0 copy-start
  141.9 1.1 fusion.8
  143.0 0.1 reshape.87
  143.1 0.1 reshape.88
  143.2 0.3 fusion.9
  143.5 0.3 multiply_cosine_fusion
  143.8 0.0 copy-start.2
  143.9 0.1 subtract_convert_fusion
  144.0 0.3 fusion
  144.2 0.0 copy-start.1
  144.2 0.6 subtract_bitcast_fusion
  144.8 0.0 copy-done
  144.8 1.3 copy.30
  146.1 0.0 copy-done.2
  146.1 0.8 copy.31
  146.9 0.0 copy-done.1
  146.9 0.8 copy.32
  (3 shorter events, 0.0 us)
Async XLA Ops:
  141.9 3.0 %copy-start = (bf16[1000,1024]{1,0:T(8,128)(2,1)S(1)}, bf16[1000,1024]{1,0:T(8,128)(2,1)}, u32[]{:S(2)}) copy-start(bf16[1000,1024]{1,0:T(8,128)(2,1)} %get-tuple-element.34) | copy-start | bytes 6144004
  143.8 2.3 %copy-start.2 = (bf16[1024,256]{1,0:T(8,128)(2,1)S(1)}, bf16[1024,256]{1,0:T(8,128)(2,1)}, u32[]{:S(2)}) copy-start(bf16[1024,256]{1,0:T(8,128)(2,1)} %get-tuple-element.35) | copy-start | bytes 1572868
  144.2 2.7 %copy-start.1 = (bf16[1024,256]{1,0:T(8,128)(2,1)S(1)}, bf16[1024,256]{1,0:T(8,128)(2,1)}, u32[]{:S(2)}) copy-start(bf16[1024,256]{1,0:T(8,128)(2,1)} %get-tuple-element.36) | copy-start | bytes 1572868

commit v6 on v5

--- a/solution.py
+++ b/solution.py
@@ -245,8 +245,8 @@
 
 
 def whole_kernel(
-    sizes, x_ref, w_ref, e_ref, q_ref, k_ref, tokens_ref,
-    ge_ref, gq_ref, gk_ref, both_ref,
+    sizes, x_ref, wq_ref, wk_ref, e_ref, q_ref, k_ref, tokens_ref,
+    ge_ref, gq_ref, gk_ref, queries_ref, keys_ref,
     x_pad, x_all, raw, w_all, e_all, o_all, total, inner_own, inner_all, grown_sum,
     lanes, squares, squares_in,
     masked, core_in, left_in, right_in, left_block, right_block, half_in, chosen_all, chosen_sum, hidden,
@@ -259,9 +259,10 @@
     new_width = sizes
     head_cols = q_ref.shape[0]
     token_rows = tokens_ref.shape[1]
-    out_slab, in_slab = w_ref.shape[1:]
+    turned = (wq_ref, wk_ref)
+    out_slab, in_slab = wq_ref.shape
     grown = (gq_ref, gk_ref)
-    per_seq = both_ref.shape[0]
+    per_seq = queries_ref.shape[0]
     cuts = row_cuts(vocab_rows, X_CUTS)
     assert len(cuts) == X_CUTS
 
@@ -272,8 +273,8 @@
         pl.semaphore_signal(barrier, inc=1, device_id=friend, device_id_type=MESH)
     local = [
         pltpu.make_async_copy(x_ref, x_pad.at[pl.ds(0, vocab_rows), :], local_sem.at[0]),
-        pltpu.make_async_copy(w_ref.at[0], w_all.at[0, place.tensor], local_sem.at[1]),
-        pltpu.make_async_copy(w_ref.at[1], w_all.at[1, place.tensor], local_sem.at[2]),
+        pltpu.make_async_copy(wq_ref, w_all.at[0, place.tensor], local_sem.at[1]),
+        pltpu.make_async_copy(wk_ref, w_all.at[1, place.tensor], local_sem.at[2]),
         pltpu.make_async_copy(q_ref, o_all.at[0], local_sem.at[3]),
         pltpu.make_async_copy(e_ref, e_all, local_sem.at[4]),
         pltpu.make_async_copy(k_ref, o_all.at[1], local_sem.at[5]),
@@ -320,7 +321,7 @@
 
     w_from = gather(
         "W", sends, lambda chunk: w_rows * in_slab * 2e-6, lambda link, chunk: 1 + chunk // W_PARTS,
-        lambda rel, chunk: w_target(rel, chunk) if any(rel) else w_view(w_ref.at[chunk // W_PARTS], chunk),
+        lambda rel, chunk: w_target(rel, chunk) if any(rel) else w_view(turned[chunk // W_PARTS], chunk),
         lambda _, rel, chunk: w_target(rel, chunk), lambda chunk: (),
     )
 
@@ -701,7 +702,7 @@
             sums = own_part[:, columns]
             for number in range(len(DP_PEERS)):
                 sums = sums + into[number].astype(jnp.float32)
-            both_ref[:, columns] = sums
+            (queries_ref, keys_ref)[matrix][...] = sums
 
     flow.task(arrivals, 1.0, add_up, rank=9, after=(("own", 0), ("own", 1)))
     order = flow.arrange()
@@ -718,7 +719,6 @@
     tokens = token_ids.shape[0]
     padded = -(-vocab_rows // 128) * 128
     per_seq = tokens // N_DP
-    turned = jnp.stack([old_query.T, old_key.T])
     anywhere = pl.BlockSpec(memory_space=pl.ANY)
     inside = pl.BlockSpec(memory_space=pltpu.VMEM)
     bf16, f32 = jnp.bfloat16, jnp.float32
@@ -729,10 +729,11 @@
             jax.ShapeDtypeStruct((vocab_rows, new_cols), bf16),
             jax.ShapeDtypeStruct((new_cols, head_cols), bf16),
             jax.ShapeDtypeStruct((new_cols, head_cols), bf16),
-            jax.ShapeDtypeStruct((per_seq, 2 * head_cols), f32),
+            jax.ShapeDtypeStruct((per_seq, head_cols), f32),
+            jax.ShapeDtypeStruct((per_seq, head_cols), f32),
         ),
-        in_specs=[anywhere] * 5 + [inside],
-        out_specs=(anywhere, inside, inside, inside),
+        in_specs=[anywhere] * 6 + [inside],
+        out_specs=(anywhere, inside, inside, inside, inside),
         scratch_shapes=[
             pltpu.VMEM((padded, slab), bf16),
             pltpu.VMEM((N_DP - 1, vocab_rows, slab), bf16),
@@ -772,7 +773,7 @@
             collective_id=1, has_side_effects=True, vmem_limit_bytes=VMEM_LIMIT
         ),
         name="grow_and_check",
-    )(old_embed, turned, expand_in, query_out, key_out, token_ids.reshape(1, tokens))
+    )(old_embed, old_query.T, old_key.T, expand_in, query_out, key_out, token_ids.reshape(1, tokens))
 
 
 def rotate(values, head_count):
@@ -810,10 +811,10 @@
 
 def on_device(token_ids, old_embed, expand_in, query_out, key_out, old_query, old_key):
     head_cols = query_out.shape[0]
-    grown_embedding, grown_query, grown_key, both = grow_and_check(
+    grown_embedding, grown_query, grown_key, queries, keys = grow_and_check(
         token_ids, old_embed, expand_in, query_out, key_out, old_query, old_key
     )
-    attention_entropy = entropy_of(both[:, :head_cols], both[:, head_cols:], head_cols // HEAD)
+    attention_entropy = entropy_of(queries, keys, head_cols // HEAD)
     return (grown_embedding, grown_query, grown_key, attention_entropy)
 
 

time: 148 us -> 147 us (level)
  other arithmetic: 3.08 us -> 0.98 us
    another operation x2 -> x1, other arithmetic: 2.18 us -> 0.08 us  [the longest x1 2.1 us: grow_and_check(): turned = jnp.stack([old_query.T, old_key.T])]
    reshape x2, local copies, waits for them, and re-layouts: 0.14 us -> 2.09 us  [rotate(): shaped = values.reshape(row_count, head_count, HEAD)]
where the time goes in v6:
time: 147 us; the launch traced here: 146 us
  Pallas kernels  139 us (95%)
  local copies, waits for them, and re-layouts  5.32 us (4%)
    pallas_call x1, Pallas kernels, grow_and_check(): pl.pallas_call(lambda *refs: whole_kernel(D_NEW, *refs), out_shape=(jax.S...  139 us

profile of v6, /device:TPU:0, one launch (start us, length us, event | category | flops | bytes accessed | tf_op | source)
XLA Modules:
  0.0 146.5 jit_solution(12097537839012736767)
XLA Ops:
  0.6 139.2 %grow_and_check.1 = (bf16[1000,1024]{1,0:T(8,128)(2,1)}, bf16[1024,256]{1,0:T(8,128)(2,1)}, bf16[1024,256]{1,0:T(8,128)(2,1)}, f32[128,256]{1,0:T(8,128)}, f32[128,256]{1,0:T(8,128)}) custom-call(bf16[1000,640]{1,0:T(8,128)(2,1)} %refs_0_.1, bf16[320,640]{1,0:T(8,128)(2,1)} %bitcast.5, bf16[320,640]{1,0:T(8,128)(2,1)} %bitcast.6, ...), custom_call_target="tpu_custom_call" | custom-call | tf_op jit(solution)/shard_map/grow_and_check/pallas_call | solution.py:726
  139.8 0.0 copy-start
  139.8 1.1 reshape.87
  141.0 1.0 reshape.88
  141.9 0.3 fusion.8
  142.3 0.3 multiply_cosine_fusion
  142.6 0.0 copy-start.2
  142.6 0.1 subtract_convert_fusion
  142.7 0.3 fusion
  143.0 0.0 copy-start.1
  143.0 0.6 subtract_bitcast_fusion
  143.6 0.0 copy-done
  143.6 1.3 copy.30
  144.9 0.0 copy-done.2
  144.9 0.8 copy.31
  145.7 0.0 copy-done.1
  145.7 0.8 copy.32
  (3 shorter events, 0.0 us)
Async XLA Ops:
  139.8 3.8 %copy-start = (bf16[1000,1024]{1,0:T(8,128)(2,1)S(1)}, bf16[1000,1024]{1,0:T(8,128)(2,1)}, u32[]{:S(2)}) copy-start(bf16[1000,1024]{1,0:T(8,128)(2,1)} %get-tuple-element.34) | copy-start | bytes 6144004
  142.6 2.3 %copy-start.2 = (bf16[1024,256]{1,0:T(8,128)(2,1)S(1)}, bf16[1024,256]{1,0:T(8,128)(2,1)}, u32[]{:S(2)}) copy-start(bf16[1024,256]{1,0:T(8,128)(2,1)} %get-tuple-element.35) | copy-start | bytes 1572868
  143.0 2.7 %copy-start.1 = (bf16[1024,256]{1,0:T(8,128)(2,1)S(1)}, bf16[1024,256]{1,0:T(8,128)(2,1)}, u32[]{:S(2)}) copy-start(bf16[1024,256]{1,0:T(8,128)(2,1)} %get-tuple-element.36) | copy-start | bytes 1572868

commit v7 on v6

--- a/solution.py
+++ b/solution.py
@@ -221,7 +221,7 @@
 LINK_RATES = {
     "y+": 0.0455, "y-": 0.0455, "z": 0.0455, "x+": 0.0455, "x-": 0.0455, "h": 0.0455, "c": 0.12, "far": 0.5, "s": 0.2,
 }
-HOP = 2.5
+HOP = 2.7
 LATENCY = {"h": 3.5}
 PEER_OVER = {
     (1, 2): ("z", "y+"), (0, 2): ("y+", "y-"), (1, 1): ("z", "y+"), (1, 3): ("z", "y-"),

time: 147 us -> 146 us (level)
  no operation moved by 1% of the time
where the time goes in v7:
time: 146 us
  Pallas kernels  139 us (95%)
  local copies, waits for them, and re-layouts  5.32 us (4%)
    pallas_call x1, Pallas kernels, grow_and_check(): pl.pallas_call(lambda *refs: whole_kernel(D_NEW, *refs), out_shape=(jax.S...  139 us

profile of v7, /device:TPU:0, one launch (start us, length us, event | category | flops | bytes accessed | tf_op | source)
XLA Modules:
  0.0 146.2 jit_solution(14367647449032870192)
XLA Ops:
  0.6 138.9 %grow_and_check.1 = (bf16[1000,1024]{1,0:T(8,128)(2,1)}, bf16[1024,256]{1,0:T(8,128)(2,1)}, bf16[1024,256]{1,0:T(8,128)(2,1)}, f32[128,256]{1,0:T(8,128)}, f32[128,256]{1,0:T(8,128)}) custom-call(bf16[1000,640]{1,0:T(8,128)(2,1)} %refs_0_.1, bf16[320,640]{1,0:T(8,128)(2,1)} %bitcast.5, bf16[320,640]{1,0:T(8,128)(2,1)} %bitcast.6, ...), custom_call_target="tpu_custom_call" | custom-call | tf_op jit(solution)/shard_map/grow_and_check/pallas_call | solution.py:726
  139.5 0.0 copy-start
  139.5 1.1 reshape.87
  140.6 1.0 reshape.88
  141.6 0.3 fusion.8
  142.0 0.3 multiply_cosine_fusion
  142.3 0.0 copy-start.2
  142.3 0.1 subtract_convert_fusion
  142.4 0.3 fusion
  142.7 0.0 copy-start.1
  142.7 0.6 subtract_bitcast_fusion
  143.3 0.0 copy-done
  143.3 1.3 copy.30
  144.6 0.0 copy-done.2
  144.6 0.8 copy.31
  145.4 0.0 copy-done.1
  145.4 0.8 copy.32
  (3 shorter events, 0.0 us)
Async XLA Ops:
  139.5 3.8 %copy-start = (bf16[1000,1024]{1,0:T(8,128)(2,1)S(1)}, bf16[1000,1024]{1,0:T(8,128)(2,1)}, u32[]{:S(2)}) copy-start(bf16[1000,1024]{1,0:T(8,128)(2,1)} %get-tuple-element.34) | copy-start | bytes 6144004
  142.3 2.3 %copy-start.2 = (bf16[1024,256]{1,0:T(8,128)(2,1)S(1)}, bf16[1024,256]{1,0:T(8,128)(2,1)}, u32[]{:S(2)}) copy-start(bf16[1024,256]{1,0:T(8,128)(2,1)} %get-tuple-element.35) | copy-start | bytes 1572868
  142.7 2.7 %copy-start.1 = (bf16[1024,256]{1,0:T(8,128)(2,1)S(1)}, bf16[1024,256]{1,0:T(8,128)(2,1)}, u32[]{:S(2)}) copy-start(bf16[1024,256]{1,0:T(8,128)(2,1)} %get-tuple-element.36) | copy-start | bytes 1572868
